TPU v7x, 32 devices: a whole 2x2x4 slice. The times are simulated.
32 devices in a mesh: rows: 32 (over z, y, x, core).
Axes of the slice: x: 2, y: 2, z: 4, core: 2. Of those that a mesh axis runs over, the one named last changes fastest.
Arguments:
- diag_noise: bfloat16 [448, 128, 128], P('rows'), may hold values from -1 to 1
- couplings: bfloat16 [448, 3, 128, 128], P('rows'), may hold values from -1 to 1
- shifts: bfloat16 [448, 128], P('rows'), may hold values from 1.5 to 3
- near_devices: int32 [448, 3], P('rows'), may hold values from 0 to 30, all different within a row; in each aligned block of 14 rows (0 to 13, 14 to 27, ...) at most 3 rows name the same one
- near_slots: int32 [448, 3], P('rows'), may hold values from 0 to 13
- vectors: float32 [32, 57344], P(None, 'rows'), may hold values from -6 to 6
Outputs:
- transformed: float32 [32, 57344], P(None, 'rows')
Inputs may be any that keep to these rules, and one draw needn't show every extreme that they name: `near_devices`: each row names three different distances. Among the 14 block rows of one device, no distance is named by more than 3 rows, and in some such group one distance is named by exactly 3 rows.
All inputs are finite; a program needn't handle non-finite values.
Results may differ from a plain program's by a relative error of at most 0.0014.
Values may be sent and summed in bfloat16 or wider, within the bound.
A program may use at most 128 MiB of HBM per device.

v0:
```python
import functools
import math

import jax
import jax.numpy as jnp
from jax import lax
from jax.experimental import pallas as pl
from jax.experimental.pallas import tpu as pltpu
from jax.sharding import PartitionSpec as P

highest = lax.Precision.HIGHEST
PANEL = 16
GROUP = 4


def split3(x):
    high = x.astype(jnp.bfloat16)
    rest = x - high.astype(jnp.float32)
    mid = rest.astype(jnp.bfloat16)
    low = (rest - mid.astype(jnp.float32)).astype(jnp.bfloat16)
    return high, mid, low


def tdot(a, b):
    return lax.dot_general(
        a, b, (((0,), (0,)), ((), ())), preferred_element_type=jnp.float32
    )


def eliminate(m, pscr, qscr, count, pad, size):
    panel = PANEL
    lane = lax.broadcasted_iota(jnp.int32, (pad, size), 1)
    for block in reversed(range(size // panel)):
        base = block * panel
        rows = [m[pl.ds(base + r, pad, stride=size), :] for r in range(panel)]
        for k in reversed(range(panel)):
            col = base + k
            here = lane == col
            if (k + 1) % GROUP == 0:
                first = k + 1 - GROUP
                tile = {
                    (i, c): jnp.broadcast_to(rows[i][:, base + c : base + c + 1], (pad, size))
                    for c in range(first, k + 1)
                    for i in range(c + 1)
                }
            inv = 1.0 / tile[k, k]
            for c in reversed(range(first, k)):
                ratio = tile[c, k] * inv
                for i in range(c + 1):
                    tile[i, c] = tile[i, c] - tile[i, k] * ratio
            pivot_row = jnp.where(here, 1.0, rows[k])
            scaled = pivot_row * inv
            for i in range(k):
                rows[i] = jnp.where(here, 0.0, rows[i]) - tile[i, k] * scaled
            if block:
                pscr[pl.ds(k * pad, pad), :] = jnp.where(
                    (lane >= base) & (lane < col), 0.0, pivot_row
                )
                qscr[pl.ds(k * pad, pad), :] = scaled
            m[pl.ds(col, pad, stride=size), :] = jnp.where(
                lane >= col, pivot_row * jnp.sqrt(inv), 0.0
            )
        if block:
            lane_m = lax.broadcasted_iota(jnp.int32, (base, size), 1)
            inside = (lane_m >= base) & (lane_m < base + panel)
            for n in range(count):
                ph, pm, plow = split3(pscr[pl.ds(n, panel, stride=pad), :])
                qh, qm, ql = split3(qscr[pl.ds(n, panel, stride=pad), :])
                right = jnp.concatenate([ph, pm, ph, plow, ph, pm], axis=0)
                left = jnp.concatenate([qh, qh, qm, qh, ql, qm], axis=0)
                update = tdot(left, right)[:base]
                spot = pl.ds(n * size, base)
                m[spot, :] = jnp.where(inside, 0.0, m[spot, :]) - update


def joined(*parts):
    return jnp.concatenate(parts, axis=-1)


def split2(x):
    high = x.astype(jnp.bfloat16)
    return high, (x - high.astype(jnp.float32)).astype(jnp.bfloat16)


def dot_nn(a, b):
    return jnp.dot(a, b, preferred_element_type=jnp.float32)


def dot_nt(a, b):
    return lax.dot_general(
        a, b, (((1,), (1,)), ((), ())), preferred_element_type=jnp.float32
    )


def inverse_kernel(d_ref, e_ref, g_ref, m, pscr, qscr):
    count, size, _ = d_ref.shape
    half = size // 2
    pad = m.shape[0] // size
    for n in range(count):
        m[pl.ds(n * size, size), :] = d_ref[n]
    for n in range(count, pad):
        m[pl.ds(n * size, size), :] = d_ref[0]
    eliminate(m, pscr, qscr, count, pad, size)
    row = lax.broadcasted_iota(jnp.int32, (half, half), 0)
    col = lax.broadcasted_iota(jnp.int32, (half, half), 1)
    row_full = lax.broadcasted_iota(jnp.int32, (size, size), 0)
    col_full = lax.broadcasted_iota(jnp.int32, (size, size), 1)
    for n in range(count):
        h, mid, low = split3(m[pl.ds(n * size, size), :])
        e = tdot(jnp.concatenate([h, h, mid], axis=0), jnp.concatenate([h, mid, h], axis=0))
        left = jnp.where(row >= col, e[:half, :half], e[half:, half:])
        e_ref[n] = joined(left, e[:half, half:]).astype(e_ref.dtype)
        diag = jnp.sum(jnp.where(row_full == col_full, e, 0.0), axis=0, keepdims=True)
        g_ref[n] = jnp.broadcast_to(diag, g_ref.shape[1:]).astype(g_ref.dtype)


def answer_kernel(capacity, served_ref, e_ref, g_ref, out_ref):
    half, size = e_ref.shape[1:]
    tail = g_ref.shape[1]
    row = lax.broadcasted_iota(jnp.int32, (tail, size), 0)

    def step(t, carry):
        tile = jnp.zeros((tail, size), jnp.float32)
        for c in range(capacity):
            source = served_ref[t * capacity + c]
            out_ref[t, pl.ds(c * half, half), :] = e_ref[source]
            tile = jnp.where(row == c, g_ref[source].astype(jnp.float32), tile)
        out_ref[t, pl.ds(capacity * half, tail), :] = tile.astype(out_ref.dtype)
        return carry

    lax.fori_loop(0, out_ref.shape[0], step, 0, unroll=8)


def factor_kernel(
    capacity, scale, target_ref, rank_ref, near_ref, c_ref, d_ref, v_ref,
    k_ref, fh_ref, fl_ref, left_ref, out_ref, m, pscr, qscr,
):
    count, size, _ = d_ref.shape
    half = size // 2
    pad = m.shape[0] // size
    tail = near_ref.shape[1] - capacity * half
    row = lax.broadcasted_iota(jnp.int32, (half, half), 0)
    col = lax.broadcasted_iota(jnp.int32, (half, half), 1)
    tail_row = lax.broadcasted_iota(jnp.int32, (tail, size), 0)

    def schur(n, carry):
        total = d_ref[n]
        for k in range(3):
            t = target_ref[3 * n + k]
            c = rank_ref[3 * n + k]
            packed = near_ref[t, pl.ds(pl.multiple_of(c * half, half), half), :]
            packed = packed.astype(jnp.float32)
            tile = near_ref[t, pl.ds(capacity * half, tail), :].astype(jnp.float32)
            diag = jnp.sum(jnp.where(tail_row == c, tile, 0.0), axis=0, keepdims=True)
            flipped = packed.T
            part = packed[:, :half]
            part_t = flipped[:half, :]
            first = jnp.where(row >= col, part, part_t)
            last = jnp.where(row < col, part, part_t)
            last = jnp.where(row == col, diag[:, half:], last)
            inverse = jnp.concatenate(
                [joined(first, packed[:, half:]), joined(flipped[half:, :], last)], axis=0
            ).astype(jnp.bfloat16)
            coupling = c_ref[n, k]
            f = dot_nn(coupling, inverse) * scale
            high, low = split2(f)
            fh_ref[n, k] = high
            fl_ref[n, k] = low
            total = total - scale * dot_nt(joined(high, low), joined(coupling, coupling))
        m[pl.ds(pl.multiple_of(n * size, size), size), :] = total
        return carry

    lax.fori_loop(0, count, schur, 0, unroll=7)
    for n in range(count, pad):
        m[pl.ds(n * size, size), :] = d_ref[0]
    eliminate(m, pscr, qscr, count, pad, size)
    out_ref[...] = jnp.zeros_like(out_ref)
    for n in range(count):
        k = m[pl.ds(n * size, size), :]
        k_ref[n] = k
        kh, kl = split2(k)
        vh, vl = split2(v_ref[:, n * size : (n + 1) * size])
        left = dot_nn(joined(vh, vh, vl), jnp.concatenate([kh, kl, kh], axis=0))
        left_ref[n] = left
        lh, ll = split2(left)
        for k in range(3):
            r = 3 * n + k
            fh, fl = fh_ref[n, k], fl_ref[n, k]
            sent = dot_nn(joined(lh, lh, ll), jnp.concatenate([fh, fl, fh], axis=0))
            out_ref[target_ref[r] * capacity + rank_ref[r]] = (-sent).astype(out_ref.dtype)


def add_arrived(total, incoming_ref, get, slots):
    count = total.shape[0] - 1
    for s in range(slots):
        wanted = incoming_ref[s]
        spot = jnp.where(wanted < 0, count, wanted)
        total[spot] = total[spot] + get(s).astype(jnp.float32)


def left_kernel(
    capacity, scale, target_ref, rank_ref, incoming_ref, arrived_ref, left_in, c_ref,
    left_ref, out_ref, total,
):
    count = left_in.shape[0]
    slots = arrived_ref.shape[0]
    total[:count] = left_in[...]
    total[count] = jnp.zeros_like(total[count])
    add_arrived(total, incoming_ref, lambda s: arrived_ref[s], slots)
    left_ref[...] = total[:count]
    for s in range(slots):
        spot = s // capacity * 2 * capacity + s % capacity
        out_ref[spot] = total[jnp.maximum(incoming_ref[s], 0)].astype(out_ref.dtype)
        out_ref[spot + capacity] = jnp.zeros_like(out_ref[spot + capacity])
    for n in range(count):
        lh, ll = split2(total[n])
        both = joined(lh, ll)
        for k in range(3):
            r = 3 * n + k
            coupling = c_ref[n, k]
            sent = scale * dot_nn(both, jnp.concatenate([coupling, coupling], axis=0))
            spot = target_ref[r] * (2 * capacity) + capacity + rank_ref[r]
            out_ref[spot] = sent.astype(out_ref.dtype)


def middle_kernel(
    capacity, scale, target_ref, rank_ref, incoming_ref, arrived_ref, own_ref, c_ref,
    middle_ref, out_ref, total,
):
    count = own_ref.shape[0]
    slots = out_ref.shape[0]
    total[count] = jnp.zeros_like(total[count])
    for n in range(count):
        near = own_ref[n]
        for k in range(3):
            r = 3 * n + k
            got = arrived_ref[target_ref[r] * (2 * capacity) + rank_ref[r]]
            near = near + scale * dot_nt(got, c_ref[n, k])
        total[n] = near
    add_arrived(
        total,
        incoming_ref,
        lambda s: arrived_ref[s // capacity * 2 * capacity + capacity + s % capacity],
        slots,
    )
    middle_ref[...] = total[:count]
    for s in range(slots):
        out_ref[s] = total[jnp.maximum(incoming_ref[s], 0)].astype(out_ref.dtype)


def final_kernel(
    capacity, target_ref, rank_ref, arrived_ref, middle_ref, k_ref, fh_ref, fl_ref, out_ref
):
    count, size, _ = k_ref.shape
    for n in range(count):
        part = middle_ref[n]
        for k in range(3):
            r = 3 * n + k
            got = arrived_ref[target_ref[r] * capacity + rank_ref[r]]
            part = part - dot_nt(joined(got, got), joined(fh_ref[n, k], fl_ref[n, k]))
        ph, plow = split2(part)
        kh, kl = split2(k_ref[n])
        out_ref[:, n * size : (n + 1) * size] = dot_nt(
            joined(ph, ph, plow), joined(kh, kl, kh)
        )


def call(kernel, scalars, arrays, shapes, scratch=()):
    smem = pl.BlockSpec(memory_space=pltpu.SMEM)
    vmem = pl.BlockSpec(memory_space=pltpu.VMEM)
    return pl.pallas_call(
        kernel,
        out_shape=[jax.ShapeDtypeStruct(shape, dtype) for shape, dtype in shapes],
        in_specs=[smem] * len(scalars) + [vmem] * len(arrays),
        out_specs=[vmem] * len(shapes),
        scratch_shapes=[pltpu.VMEM(shape, jnp.float32) for shape in scratch],
    )(*scalars, *arrays)


def build_diag(noise_block, shift_block, factor):
    noise_block = noise_block.astype(jnp.float32) * factor
    symmetric = (noise_block + jnp.swapaxes(noise_block, -1, -2)) * 0.5
    eye_block = jnp.eye(noise_block.shape[-1], dtype=jnp.float32)
    return symmetric + shift_block.astype(jnp.float32)[..., :, None] * eye_block


def exchange(x, dev_count):
    shape = x.shape
    x = x.reshape(dev_count, -1, *shape[1:])
    x = lax.all_to_all(x, "rows", split_axis=0, concat_axis=0, tiled=True)
    return x.reshape(shape)


def body(diag_noise, couplings, shifts, near_devices, near_slots, vectors):
    dev_count = lax.axis_size("rows")
    my_index = lax.axis_index("rows")
    row_count = diag_noise.shape[0]
    block_size = diag_noise.shape[1]
    vec_count = vectors.shape[0]
    capacity = 3 * row_count // (dev_count - 1) + 2
    slot_total = dev_count * capacity
    factor = 0.5 / math.sqrt(block_size)
    coupling_factor = 0.4 / math.sqrt(block_size)
    target = ((my_index - 1 - near_devices) % dev_count).reshape(-1)
    device_onehot = (target[:, None] == jnp.arange(dev_count, dtype=jnp.int32)[None, :]).astype(
        jnp.int32
    )
    running = jnp.cumsum(device_onehot, axis=0) - 1
    rank = jnp.sum(running * device_onehot, axis=1)
    position = target * capacity + rank
    hit = position[None, :] == jnp.arange(slot_total, dtype=jnp.int32)[:, None]
    asked_slots = jnp.sum(jnp.where(hit, near_slots.reshape(1, -1) + 1, 0), axis=1) - 1
    incoming = exchange(asked_slots, dev_count)
    served = jnp.maximum(incoming, 0)
    diag_own = build_diag(diag_noise, shifts, factor)

    bf16, f32 = jnp.bfloat16, jnp.float32
    half = block_size // 2
    tail = 16
    pad = -(-row_count // 8) * 8
    work = ((pad * block_size, block_size),) + ((PANEL * pad, block_size),) * 2
    packed, diags = call(
        inverse_kernel,
        (),
        (diag_own,),
        (((row_count, half, block_size), bf16), ((row_count, tail, block_size), bf16)),
        work,
    )
    (answer,) = call(
        functools.partial(answer_kernel, capacity),
        (served,),
        (packed, diags),
        (((dev_count, capacity * half + tail, block_size), bf16),),
    )
    near = exchange(answer, dev_count)
    rows_shape = (row_count, vec_count, block_size)
    total_shape = ((row_count + 1, vec_count, block_size),)
    slots_shape = (slot_total, vec_count, block_size)
    f_shape = (row_count, 3, block_size, block_size)
    k_all, f_high, f_low, left, outgoing = call(
        functools.partial(factor_kernel, capacity, coupling_factor),
        (target, rank),
        (near, couplings, diag_own, vectors),
        (
            ((row_count, block_size, block_size), f32),
            (f_shape, bf16),
            (f_shape, bf16),
            (rows_shape, f32),
            (slots_shape, bf16),
        ),
        work,
    )
    arrived = exchange(outgoing, dev_count)
    left, outgoing = call(
        functools.partial(left_kernel, capacity, coupling_factor),
        (target, rank, incoming),
        (arrived, left, couplings),
        ((rows_shape, f32), ((2 * slot_total, vec_count, block_size), bf16)),
        total_shape,
    )
    arrived = exchange(outgoing, dev_count)
    own = jnp.einsum("rva,rab->rvb", left, diag_own, precision=highest)
    middle, outgoing = call(
        functools.partial(middle_kernel, capacity, coupling_factor),
        (target, rank, incoming),
        (arrived, own, couplings),
        ((rows_shape, f32), (slots_shape, bf16)),
        total_shape,
    )
    arrived = exchange(outgoing, dev_count)
    (result,) = call(
        functools.partial(final_kernel, capacity),
        (target, rank),
        (arrived, middle, k_all, f_high, f_low),
        ((vectors.shape, f32),),
    )
    return result


def solution(mesh):
    return jax.shard_map(
        body,
        mesh=mesh,
        in_specs=(
            P("rows", None, None),
            P("rows", None, None, None),
            P("rows", None),
            P("rows", None),
            P("rows", None),
            P(None, "rows"),
        ),
        out_specs=P(None, "rows"),
        check_vma=False,
    )
```

profile of v0, /device:TPU:0, one launch (start us, length us, event | category | flops | bytes accessed | tf_op | source)
XLA Modules:
  0.0 199.9 jit_solution(11885102189549999676)
XLA Ops:
  0.0 0.7 broadcast_add_fusion
  0.7 0.1 copy.22
  0.8 0.1 add.49
  0.9 0.7 add_select_fusion
  1.6 0.1 copy.21
  1.7 0.1 reshape.75.target_ref
  1.8 0.0 copy-start.3
  1.8 0.1 fusion.3
  1.8 0.1 reduce_window_sum.11
  1.9 0.2 select_reduce_fusion.1.rank_ref
  2.1 0.0 copy-start.4
  2.1 0.1 select_reduce_fusion
  2.2 0.7 sub.24
  2.9 7.3 %all-to-all-start = ((s32[32,1,3]{2,1,0:T(1,128)}), s32[32,1,3]{2,1,0:T(1,128)S(1)}, u32[]{:S(2)}, u32[]{:S(2)}) async-start(s32[32,1,3]{2,1,0:T(1,128)} %bitcast), calls=%async_computation | async-start | bytes 32768 | tf_op jit(solution)/shard_map/all_to_all | solution.py:290
  10.3 0.7 convert_element_type.18
  11.0 1.3 copy.24
  12.2 0.1 convert_multiply_fusion
  12.4 0.3 copy.25
  12.7 0.0 copy-done.3
  12.7 0.0 copy-done.4
  12.7 1.2 fusion.1.d_ref
  13.9 9.5 %shard_map.64 = (bf16[14,64,128]{2,1,0:T(8,128)(2,1)}, bf16[14,16,128]{2,1,0:T(8,128)(2,1)}) custom-call(f32[14,128,128]{2,1,0:T(8,128)} %fusion.1.d_ref), custom_call_target="tpu_custom_call" | custom-call | tf_op jit(solution)/shard_map/pallas_call | solution.py:271
  23.4 0.0 all-to-all-done
  23.4 0.5 broadcast.48
  23.9 0.7 reduce.3
  24.6 0.1 reshape.76.incoming_ref
  24.7 0.0 copy-start.5
  24.7 0.5 broadcast_maximum_fusion.served_ref
  25.3 2.3 %shard_map.65 = bf16[32,208,128]{2,1,0:T(8,128)(2,1)} custom-call(s32[96]{0:T(128)} %broadcast_maximum_fusion.served_ref, bf16[14,64,128]{2,1,0:T(8,128)(2,1)} %get-tuple-element.16.e_ref, bf16[14,16,128]{2,1,0:T(8,128)(2,1)} %get-tuple-element.17.g_ref), custom_call_target="tpu_custom_call" | custom-call | tf_op jit(solution)/shard_map/pallas_call | solution.py:271
  27.6 46.4 %all_to_all.26 = bf16[32,1,208,128]{3,2,1,0:T(8,128)(2,1)} all-to-all(bf16[32,1,208,128]{3,2,1,0:T(8,128)(2,1)} %bitcast.20), channel_id=1, replica_groups=mesh['rows'=32] {'rows'}, dimensions={0} | all-to-all | bytes 3407872 | tf_op jit(solution)/shard_map/all_to_all | solution.py:290
  74.0 0.0 copy-done.5
  74.0 20.6 %shard_map.66 = (f32[14,128,128]{2,1,0:T(8,128)}, bf16[14,3,128,128]{3,2,1,0:T(8,128)(2,1)}, bf16[14,3,128,128]{3,2,1,0:T(8,128)(2,1)}, f32[14,32,128]{2,1,0:T(8,128)}, bf16[96,32,128]{2,1,0:T(8,128)(2,1)}) custom-call(s32[42]{0:T(128)} %copy-done.3, s32[42]{0:T(128)} %copy-done.4, bf16[32,208,128]{2,1,0:T(8,128)(2,1)} %bitcast.19, ...), custom_call_target="tpu_custom_call" | custom-call | tf_op jit(solution)/shard_map/pallas_call | solution.py:271
  94.6 24.1 %all_to_all.27 = bf16[32,3,32,128]{3,2,1,0:T(8,128)(2,1)} all-to-all(bf16[32,3,32,128]{3,2,1,0:T(8,128)(2,1)} %bitcast.25), channel_id=1, replica_groups=mesh['rows'=32] {'rows'}, dimensions={0} | all-to-all | bytes 1572864 | tf_op jit(solution)/shard_map/all_to_all | solution.py:290
  118.7 4.0 %shard_map.67 = (f32[14,32,128]{2,1,0:T(8,128)}, bf16[192,32,128]{2,1,0:T(8,128)(2,1)}) custom-call(s32[42]{0:T(128)} %copy-done.3, s32[42]{0:T(128)} %copy-done.4, s32[96]{0:T(128)} %copy-done.5, bf16[96,32,128]{2,1,0:T(8,128)(2,1)} %bitcast.22, f32[14,32,128]{2,1,0:T(8,128)} %get-tuple-element.19.left_in, bf16[14,3,128,128]{3,2,1,0:T(8,128)(2,1)} %c_ref.5), custom_call_target="tpu_custom_call" | custom-call | tf_op jit(solution)/shard_map/pallas_call | solution.py:271
  122.7 0.0 copy-start
  122.7 0.0 copy-start.2
  122.7 3.8 %all-to-all-start.3 = ((bf16[32,6,32,128]{3,2,1,0:T(8,128)(2,1)}), bf16[32,6,32,128]{3,2,1,0:T(8,128)(2,1)S(1)}, u32[]{:S(2)}, u32[]{:S(2)}) async-start(bf16[32,6,32,128]{3,2,1,0:T(8,128)(2,1)} %bitcast.24), calls=%async_computation.3 | async-start | bytes 3145728 | tf_op jit(solution)/shard_map/all_to_all | solution.py:290
  126.6 0.0 copy-done
  126.6 0.0 copy-done.2
  126.6 1.6 fusion.5.own_ref
  128.2 35.9 %all-to-all-done.3 = bf16[32,6,32,128]{3,2,1,0:T(8,128)(2,1)S(1)} async-done(((bf16[32,6,32,128]{3,2,1,0:T(8,128)(2,1)}), bf16[32,6,32,128]{3,2,1,0:T(8,128)(2,1)S(1)}, u32[]{:S(2)}, u32[]{:S(2)}) %all-to-all-start.3) | async-done | bytes 1572896 | tf_op jit(solution)/shard_map/all_to_all | solution.py:290
  164.0 0.0 copy-start.1
  164.1 1.2 copy-done.1
  165.2 4.3 %shard_map.68 = (f32[14,32,128]{2,1,0:T(8,128)}, bf16[96,32,128]{2,1,0:T(8,128)(2,1)}) custom-call(s32[42]{0:T(128)} %copy-done.3, s32[42]{0:T(128)} %copy-done.4, s32[96]{0:T(128)} %copy-done.5, bf16[192,32,128]{2,1,0:T(8,128)(2,1)} %bitcast.21, f32[14,32,128]{2,1,0:T(8,128)} %fusion.5.own_ref, bf16[14,3,128,128]{3,2,1,0:T(8,128)(2,1)} %c_ref.5), custom_call_target="tpu_custom_call" | custom-call | tf_op jit(solution)/shard_map/pallas_call | solution.py:271
  169.6 24.4 %all_to_all.28 = bf16[32,3,32,128]{3,2,1,0:T(8,128)(2,1)} all-to-all(bf16[32,3,32,128]{3,2,1,0:T(8,128)(2,1)} %bitcast.26), channel_id=1, replica_groups=mesh['rows'=32] {'rows'}, dimensions={0} | all-to-all | bytes 1572864 | tf_op jit(solution)/shard_map/all_to_all | solution.py:290
  194.0 5.9 %shard_map.69 = f32[32,1792]{1,0:T(8,128)} custom-call(s32[42]{0:T(128)} %copy-done.3, s32[42]{0:T(128)} %copy-done.4, bf16[96,32,128]{2,1,0:T(8,128)(2,1)} %bitcast.23, f32[14,32,128]{2,1,0:T(8,128)} %get-tuple-element.23.middle_ref, f32[14,128,128]{2,1,0:T(8,128)} %get-tuple-element.24.k_ref, bf16[14,3,128,128]{3,2,1,0:T(8,128)(2,1)} %get-tuple-element.25.fh_ref, ...), custom_call_target="tpu_custom_call" | custom-call | tf_op jit(solution)/shard_map/pallas_call | solution.py:271
  (3 shorter events, 0.0 us)
Async XLA Ops:
  1.8 10.9 %copy-start.3 = (s32[42]{0:T(128)}, s32[42]{0:T(128)S(1)}, u32[]{:S(2)}) copy-start(s32[42]{0:T(128)S(1)} %reshape.75.target_ref) | copy-start | bytes 508
  2.1 10.6 %copy-start.4 = (s32[42]{0:T(128)}, s32[42]{0:T(128)S(1)}, u32[]{:S(2)}) copy-start(s32[42]{0:T(128)S(1)} %select_reduce_fusion.1.rank_ref) | copy-start | bytes 508
  2.9 20.5 %all-to-all-start = ((s32[32,1,3]{2,1,0:T(1,128)}), s32[32,1,3]{2,1,0:T(1,128)S(1)}, u32[]{:S(2)}, u32[]{:S(2)}) async-start(s32[32,1,3]{2,1,0:T(1,128)} %bitcast), calls=%async_computation | async-start | bytes 32768 | tf_op jit(solution)/shard_map/all_to_all | solution.py:290
  24.7 49.3 %copy-start.5 = (s32[96]{0:T(128)}, s32[96]{0:T(128)S(1)}, u32[]{:S(2)}) copy-start(s32[96]{0:T(128)S(1)} %reshape.76.incoming_ref) | copy-start | bytes 1156
  122.7 3.9 %copy-start = (f32[14,128,128]{2,1,0:T(8,128)S(1)}, f32[14,128,128]{2,1,0:T(8,128)}, u32[]{:S(2)}) copy-start(f32[14,128,128]{2,1,0:T(8,128)} %fusion.1.d_ref) | copy-start | bytes 2752516
  122.7 3.9 %copy-start.2 = (f32[14,32,128]{2,1,0:T(8,128)S(1)}, f32[14,32,128]{2,1,0:T(8,128)}, u32[]{:S(2)}) copy-start(f32[14,32,128]{2,1,0:T(8,128)} %get-tuple-element.21) | copy-start | bytes 688132
  122.7 41.3 %all-to-all-start.3 = ((bf16[32,6,32,128]{3,2,1,0:T(8,128)(2,1)}), bf16[32,6,32,128]{3,2,1,0:T(8,128)(2,1)S(1)}, u32[]{:S(2)}, u32[]{:S(2)}) async-start(bf16[32,6,32,128]{3,2,1,0:T(8,128)(2,1)} %bitcast.24), calls=%async_computation.3 | async-start | bytes 3145728 | tf_op jit(solution)/shard_map/all_to_all | solution.py:290
  164.0 1.2 copy-start.1
where the time goes:
time: 201 us; the launch traced here: 200 us
  blocking collectives  95 us (47%)
  Pallas kernels  46.6 us (23%)
  waiting for transfers between devices  35.9 us (18%)
  starting transfers between devices  11.2 us (6%)
  other arithmetic  5.01 us (2%)
  local copies, waits for them, and re-layouts  4.48 us (2%)
    all_to_all x3, blocking collectives, exchange(): x = lax.all_to_all(x, 'rows', split_axis=0, concat_axis=0, tiled=True)  95 us
    pallas_call x6, Pallas kernels, call(): pl.pallas_call(kernel, out_shape=[jax.ShapeDtypeStruct(shape, dtype) for...  46.6 us
    all_to_all x2, waiting for transfers between devices, exchange(): x = lax.all_to_all(x, 'rows', split_axis=0, concat_axis=0, tiled=True)  35.9 us
    all_to_all x2, starting transfers between devices, exchange(): x = lax.all_to_all(x, 'rows', split_axis=0, concat_axis=0, tiled=True)  11.2 us
  transfers between devices with their start and end apart: 2, of which 1 were waited for; matrix products, arithmetic and copies ran while one was open for 3% of the time, Pallas kernels for 5%

commit v1 on v0

v1 whole, which is shorter than its diff:
```python
import functools
import math

import jax
import jax.numpy as jnp
from jax import lax
from jax.experimental import pallas as pl
from jax.experimental.pallas import tpu as pltpu
from jax.sharding import PartitionSpec as P

PANEL = 16
GROUP = 4
LAYERS = 4
TAIL = 16
MESH = pl.DeviceIdType.MESH
bf16, f32 = jnp.bfloat16, jnp.float32


def split2(x):
    high = x.astype(bf16)
    return high, (x - high.astype(f32)).astype(bf16)


def joined(*parts):
    return jnp.concatenate(parts, axis=-1)


def tdot(a, b):
    return lax.dot_general(a, b, (((0,), (0,)), ((), ())), preferred_element_type=f32)


def dot_nn(a, b):
    return jnp.dot(a, b, preferred_element_type=f32)


def dot_nt(a, b):
    return lax.dot_general(a, b, (((1,), (1,)), ((), ())), preferred_element_type=f32)


def eliminate(m, pscr, qscr, count, pad, size):
    panel = PANEL
    lane = lax.broadcasted_iota(jnp.int32, (pad, size), 1)
    for block in reversed(range(size // panel)):
        base = block * panel
        rows = [m[pl.ds(base + r, pad, stride=size), :] for r in range(panel)]
        for k in reversed(range(panel)):
            col = base + k
            here = lane == col
            if (k + 1) % GROUP == 0:
                first = k + 1 - GROUP
                tile = {
                    (i, c): jnp.broadcast_to(rows[i][:, base + c : base + c + 1], (pad, size))
                    for c in range(first, k + 1)
                    for i in range(c + 1)
                }
            inv = 1.0 / tile[k, k]
            for c in reversed(range(first, k)):
                ratio = tile[c, k] * inv
                for i in range(c + 1):
                    tile[i, c] = tile[i, c] - tile[i, k] * ratio
            pivot_row = jnp.where(here, 1.0, rows[k])
            scaled = pivot_row * inv
            for i in range(k):
                rows[i] = jnp.where(here, 0.0, rows[i]) - tile[i, k] * scaled
            if block:
                pscr[pl.ds(k * pad, pad), :] = jnp.where(
                    (lane >= base) & (lane < col), 0.0, pivot_row
                )
                qscr[pl.ds(k * pad, pad), :] = scaled
            m[pl.ds(col, pad, stride=size), :] = jnp.where(
                lane >= col, pivot_row * jnp.sqrt(inv), 0.0
            )
        if block:
            lane_m = lax.broadcasted_iota(jnp.int32, (base, size), 1)
            inside = (lane_m >= base) & (lane_m < base + panel)
            for n in range(count):
                ph, plow = split2(pscr[pl.ds(n, panel, stride=pad), :])
                qh, qlow = split2(qscr[pl.ds(n, panel, stride=pad), :])
                right = jnp.concatenate([ph, plow, ph], axis=0)
                left = jnp.concatenate([qh, qh, qlow], axis=0)
                update = tdot(left, right)[:base]
                spot = pl.ds(n * size, base)
                m[spot, :] = jnp.where(inside, 0.0, m[spot, :]) - update


def inverse_kernel(factor, noise_ref, shift_ref, d_ref, e_ref, packed_ref, tail_ref, m, pscr, qscr):
    count, size, _ = noise_ref.shape
    half = size // 2
    pad = m.shape[0] // size
    row_full = lax.broadcasted_iota(jnp.int32, (size, size), 0)
    col_full = lax.broadcasted_iota(jnp.int32, (size, size), 1)
    on_diag = row_full == col_full
    for n in range(count):
        noise = noise_ref[n].astype(f32)
        d = (noise + noise.T) * (0.5 * factor)
        d = d + jnp.where(on_diag, shift_ref[pl.ds(n, 1), :], 0.0)
        d_ref[n] = d
        m[pl.ds(n * size, size), :] = d
        if n < pad - count:
            m[pl.ds((count + n) * size, size), :] = d
    eliminate(m, pscr, qscr, count, pad, size)
    row = lax.broadcasted_iota(jnp.int32, (half, half), 0)
    col = lax.broadcasted_iota(jnp.int32, (half, half), 1)
    tail_row = lax.broadcasted_iota(jnp.int32, (TAIL, size), 0)
    tile = jnp.zeros((TAIL, size), f32)
    for n in range(count):
        h, low = split2(m[pl.ds(n * size, size), :])
        e = tdot(jnp.concatenate([h, h, low], axis=0), jnp.concatenate([h, low, h], axis=0))
        e_ref[n] = e.astype(bf16)
        left = jnp.where(row >= col, e[:half, :half], e[half:, half:])
        packed_ref[n] = joined(left, e[:half, half:]).astype(bf16)
        diag = jnp.sum(jnp.where(on_diag, e, 0.0), axis=0, keepdims=True)
        tile = jnp.where(tail_row == n, diag, tile)
    tail_ref[...] = tile.astype(bf16)


def factor_kernel(
    capacity, scale, target_ref, rank_ref, near_ref, c_ref, d_ref, v_ref,
    k_ref, u_ref, out_ref, m, pscr, qscr,
):
    count, size, _ = d_ref.shape
    vec = v_ref.shape[0]
    half = size // 2
    pad = m.shape[0] // size
    row = lax.broadcasted_iota(jnp.int32, (half, half), 0)
    col = lax.broadcasted_iota(jnp.int32, (half, half), 1)
    tail_row = lax.broadcasted_iota(jnp.int32, (TAIL, size), 0)

    def schur(n, carry):
        fs, cs = [], []
        for k in range(3):
            t = target_ref[3 * n + k]
            c = rank_ref[3 * n + k]
            packed = near_ref[t, pl.ds(pl.multiple_of(c * half, half), half), :]
            packed = packed.astype(f32)
            tile = near_ref[t, pl.ds(capacity * half, TAIL), :].astype(f32)
            diag = jnp.sum(jnp.where(tail_row == c, tile, 0.0), axis=0, keepdims=True)
            flipped = packed.T
            part = packed[:, :half]
            part_t = flipped[:half, :]
            first = jnp.where(row >= col, part, part_t)
            last = jnp.where(row < col, part, part_t)
            last = jnp.where(row == col, diag[:, half:], last)
            inverse = jnp.concatenate(
                [joined(first, packed[:, half:]), joined(flipped[half:, :], last)], axis=0
            ).astype(bf16)
            coupling = c_ref[n, k]
            fs.append((dot_nn(coupling, inverse) * (scale * scale)).astype(bf16))
            cs.append(coupling)
        total = d_ref[n] - dot_nt(joined(*fs), joined(*cs))
        m[pl.ds(pl.multiple_of(n * size, size), size), :] = total
        return carry

    lax.fori_loop(0, count, schur, 0, unroll=7)
    for n in range(count, pad):
        m[pl.ds(n * size, size), :] = d_ref[0]
    eliminate(m, pscr, qscr, count, pad, size)
    out_ref[...] = jnp.zeros_like(out_ref)
    for n in range(count):
        k = m[pl.ds(n * size, size), :]
        k_ref[n] = k
        kh, kl = split2(k)
        vh, vl = split2(v_ref[:, n * size : (n + 1) * size])
        u = dot_nn(joined(vh, vh, vl), jnp.concatenate([kh, kl, kh], axis=0))
        u_ref[n] = u
        low = (u * scale).astype(bf16)
        for k in range(3):
            r = 3 * n + k
            spot = pl.ds(pl.multiple_of(rank_ref[r] * vec, vec), vec)
            out_ref[target_ref[r], spot, :] = dot_nn(low, c_ref[n, k]).astype(bf16)


def left_kernel(
    capacity, scale, target_ref, rank_ref, w_ref, u_ref, e_ref, c_ref,
    p_ref, left_ref, out_ref,
):
    count, vec, _ = u_ref.shape
    out_ref[...] = jnp.zeros_like(out_ref)
    for n in range(count):
        p = dot_nn(w_ref[pl.ds(n * vec, vec), :].astype(bf16), e_ref[n])
        p_ref[n] = p
        left_ref[n] = (u_ref[n] - p).astype(bf16)
        low = (p * scale).astype(bf16)
        for k in range(3):
            r = 3 * n + k
            spot = pl.ds(pl.multiple_of(rank_ref[r] * vec, vec), vec)
            out_ref[target_ref[r], spot, :] = dot_nn(low, c_ref[n, k]).astype(bf16)


def pulled(n, capacity, scale, target_ref, rank_ref, near_ref, c_ref):
    vec = near_ref.shape[1] // capacity
    got, cs = [], []
    for k in range(3):
        r = 3 * n + k
        spot = pl.ds(pl.multiple_of(rank_ref[r] * vec, vec), vec)
        got.append(near_ref[target_ref[r], spot, :])
        cs.append(c_ref[n, k])
    return scale * dot_nt(joined(*got), joined(*cs))


def middle_kernel(
    capacity, scale, target_ref, rank_ref, near_ref, pushed_ref, u_ref, p_ref, e_ref, d_ref, c_ref,
    t_ref, rest_ref,
):
    count, vec, _ = u_ref.shape
    for n in range(count):
        pushed = pushed_ref[pl.ds(n * vec, vec), :]
        q = pulled(n, capacity, scale, target_ref, rank_ref, near_ref, c_ref) - pushed
        t = p_ref[n] + dot_nn(q.astype(bf16), e_ref[n])
        t_ref[n] = t.astype(bf16)
        uh, ul = split2(u_ref[n])
        dh, dl = split2(d_ref[n])
        own = dot_nn(joined(uh, uh, ul), jnp.concatenate([dh, dl, dh], axis=0))
        rest_ref[n] = own - pushed


def final_kernel(capacity, scale, target_ref, rank_ref, near_ref, rest_ref, k_ref, c_ref, out_ref):
    count, size, _ = k_ref.shape
    for n in range(count):
        part = rest_ref[n] - pulled(n, capacity, scale, target_ref, rank_ref, near_ref, c_ref)
        ph, plow = split2(part)
        kh, kl = split2(k_ref[n])
        out_ref[:, n * size : (n + 1) * size] = dot_nt(
            joined(ph, ph, plow), joined(kh, kl, kh)
        )


def comm_kernel(geometry, pull, push, *refs):
    total, layers, capacity, count = geometry
    plane = total // layers
    refs = list(refs)
    take = lambda k: [refs.pop(0) for _ in range(k)]
    (table_ref,) = take(1)
    if pull:
        height, tail = pull
        parts = 2 if tail else 1
        own_ref = take(parts)
    if push:
        lanes_ref, out_ref = take(2)
    if pull:
        (near_ref,) = take(1)
    if push:
        (sum_ref,) = take(1)
    if pull:
        zbuf = [take(parts) for _ in range(layers - 1)]
        (send_ref,) = take(1)
    if push:
        arrive_ref, zout_ref, zin_ref = take(3)
    if pull:
        pz_send, pz_recv, pp_send, pp_recv = take(4)
    if push:
        sz_send, sz_recv, sp_send, sp_recv = take(4)
    me = lax.axis_index("rows")
    z = me // plane
    q = lax.rem(me, plane)
    zs = [jnp.bitwise_xor(z, o) for o in range(layers)]
    qs = [jnp.bitwise_xor(q, e) for e in range(plane)]

    barrier = pltpu.get_barrier_semaphore()
    partners = [zs[o] * plane + q for o in range(1, layers)]
    partners += [z * plane + qs[e] for e in range(1, plane)]
    for device in partners:
        pl.semaphore_signal(barrier, inc=1, device_id=(device,), device_id_type=MESH)

    def remote(src, dst, send, recv, device):
        return pltpu.make_async_remote_copy(
            src_ref=src, dst_ref=dst, send_sem=send, recv_sem=recv,
            device_id=(device,), device_id_type=MESH,
        )

    if pull:
        tail_row = lax.broadcasted_iota(jnp.int32, (TAIL, 128), 0)
        pull_z = [
            [
                remote(
                    own_ref[i], zbuf[o - 1][i], pz_send.at[o - 1, i], pz_recv.at[o - 1, i],
                    zs[o] * plane + q,
                )
                for i in range(parts)
            ]
            for o in range(1, layers)
        ]
        pull_p = {
            (o, e): remote(
                send_ref.at[o * plane + e], near_ref.at[zs[o] * plane + q],
                pp_send.at[o, e], pp_recv.at[o, e], z * plane + qs[e],
            )
            for o in range(layers)
            for e in range(1, plane)
        }

        def pack(o, e):
            source = own_ref if o == 0 else zbuf[o - 1]
            target, slot = (near_ref, zs[o] * plane + q) if e == 0 else (send_ref, o * plane + e)
            tile = jnp.zeros((TAIL, 128), f32)
            if tail:
                every = source[1][...].astype(f32)
            for c in range(capacity):
                index = jnp.maximum(table_ref[(qs[e] * layers + zs[o]) * capacity + c], 0)
                target[slot, pl.ds(c * height, height), :] = source[0][index]
                if tail:
                    line = jnp.sum(jnp.where(tail_row == index, every, 0.0), axis=0, keepdims=True)
                    tile = jnp.where(tail_row == c, line, tile)
            if tail:
                target[slot, pl.ds(capacity * height, TAIL), :] = tile.astype(bf16)

        for e in range(1, plane):
            pack(0, e)
    if push:
        step = out_ref.shape[1]
        vec = step // capacity
        width = plane * step
        push_p = {
            (o, e): remote(
                out_ref.at[zs[o] * plane + qs[e]], arrive_ref.at[zs[o], pl.ds(pl.multiple_of(q * step, step), step)],
                sp_send.at[o, e], sp_recv.at[o, e], z * plane + qs[e],
            )
            for o in range(layers)
            for e in range(1, plane)
        }
        push_z = [
            remote(zout_ref.at[o - 1], zin_ref.at[o - 1], sz_send.at[o - 1], sz_recv.at[o - 1], zs[o] * plane + q)
            for o in range(1, layers)
        ]

        def gather_sum(o):
            lanes = lanes_ref[pl.ds(zs[o], 1), :]
            row = lax.broadcasted_iota(jnp.int32, (vec, width), 0)
            col = lax.broadcasted_iota(jnp.int32, (vec, width), 1)
            same = row == lax.rem(col, vec)
            pick = jnp.concatenate(
                [jnp.where(same & (lanes == k), 1.0, 0.0).astype(bf16) for k in range(count)], axis=0
            )
            return dot_nn(pick, arrive_ref[zs[o]])

    pl.semaphore_wait(barrier, len(partners))
    if pull:
        for o in reversed(range(1, layers)):
            for copy in pull_z[o - 1]:
                copy.start()
    if push:
        for o in list(range(1, layers)) + [0]:
            for e in reversed(range(1, plane)):
                push_p[o, e].start()
        for o in range(layers):
            here = pl.ds(pl.multiple_of(q * step, step), step)
            arrive_ref[zs[o], here, :] = out_ref[zs[o] * plane + q]
    if pull:
        for e in reversed(range(1, plane)):
            pull_p[0, e].start()
        pack(0, 0)
    for o in range(1, layers):
        if push:
            for e in range(1, plane):
                push_p[o, e].wait_recv()
            zout_ref[o - 1] = gather_sum(o).astype(bf16)
            push_z[o - 1].start()
        if pull:
            for copy in pull_z[o - 1]:
                copy.wait_recv()
            for e in reversed(range(1, plane)):
                pack(o, e)
                pull_p[o, e].start()
            pack(o, 0)
    if push:
        for e in range(1, plane):
            push_p[0, e].wait_recv()
        total_sum = gather_sum(0)
        for o in range(1, layers):
            push_z[o - 1].wait_recv()
            total_sum = total_sum + zin_ref[o - 1].astype(f32)
        sum_ref[...] = total_sum
        for o in range(1, layers):
            push_z[o - 1].wait_send()
        for copy in push_p.values():
            copy.wait_send()
    if pull:
        for copy in pull_p.values():
            copy.wait_recv()
        for copy in pull_p.values():
            copy.wait_send()
        for copies in pull_z:
            for copy in copies:
                copy.wait_send()


def communicate(geometry, number, table, pull=None, own=None, push=None, lanes=None):
    total, layers, capacity, count = geometry
    plane = total // layers
    smem = pl.BlockSpec(memory_space=pltpu.SMEM)
    vmem = pl.BlockSpec(memory_space=pltpu.VMEM)
    args, specs, shapes, scratch, sems = [table], [smem], [], [], []
    dma = pltpu.SemaphoreType.DMA
    if pull:
        args += own
        specs += [vmem] * len(own)
        height, tail = pull
        block = (capacity * height + tail, own[0].shape[-1])
        shapes += [jax.ShapeDtypeStruct((total,) + block, bf16)]
        scratch += [pltpu.VMEM(part.shape, bf16) for part in own] * (layers - 1)
        scratch += [pltpu.VMEM((total,) + block, bf16)]
        sems += [dma((layers - 1, len(own)))] * 2 + [dma((layers, plane))] * 2
    if push is not None:
        args += [lanes, push]
        specs += [vmem, vmem]
        step, size = push.shape[1:]
        height = step // capacity * count
        shapes += [jax.ShapeDtypeStruct((height, size), f32)]
        scratch += [pltpu.VMEM((layers, plane * step, size), push.dtype)]
        scratch += [pltpu.VMEM((layers - 1, height, size), push.dtype)] * 2
        sems += [dma((layers - 1,))] * 2 + [dma((layers, plane))] * 2
    return pl.pallas_call(
        functools.partial(comm_kernel, geometry, pull, push is not None),
        out_shape=shapes,
        in_specs=specs,
        out_specs=[vmem] * len(shapes),
        scratch_shapes=scratch + sems,
        compiler_params=pltpu.CompilerParams(collective_id=number, has_side_effects=True),
    )(*args)


def call(kernel, scalars, arrays, shapes, scratch=()):
    smem = pl.BlockSpec(memory_space=pltpu.SMEM)
    vmem = pl.BlockSpec(memory_space=pltpu.VMEM)
    return pl.pallas_call(
        kernel,
        out_shape=[jax.ShapeDtypeStruct(shape, dtype) for shape, dtype in shapes],
        in_specs=[smem] * len(scalars) + [vmem] * len(arrays),
        out_specs=[vmem] * len(shapes),
        scratch_shapes=[pltpu.VMEM(shape, f32) for shape in scratch],
    )(*scalars, *arrays)


def body(diag_noise, couplings, shifts, near_devices, near_slots, vectors):
    dev_count = lax.axis_size("rows")
    my_index = lax.axis_index("rows")
    row_count, block_size = diag_noise.shape[:2]
    vec_count = vectors.shape[0]
    capacity = 3 * row_count // (dev_count - 1) + 2
    layers = LAYERS
    plane = dev_count // layers
    factor = 0.5 / math.sqrt(block_size)
    scale = 0.4 / math.sqrt(block_size)
    geometry = (dev_count, layers, capacity, row_count)

    target = ((my_index - 1 - near_devices) % dev_count).reshape(-1)
    device_onehot = (target[:, None] == jnp.arange(dev_count, dtype=jnp.int32)[None, :]).astype(
        jnp.int32
    )
    running = jnp.cumsum(device_onehot, axis=0) - 1
    rank = jnp.sum(running * device_onehot, axis=1)
    position = (target % plane * layers + target // plane) * capacity + rank
    hit = position[None, :] == jnp.arange(dev_count * capacity, dtype=jnp.int32)[:, None]
    asked = jnp.sum(jnp.where(hit, near_slots.reshape(1, -1) + 1, 0), axis=1) - 1
    groups = [[i * plane + j for j in range(plane)] for i in range(layers)]
    table = lax.all_to_all(
        asked.reshape(plane, layers * capacity), "rows", 0, 0,
        axis_index_groups=groups, tiled=True,
    ).reshape(-1)
    lanes = table.reshape(plane, layers, capacity).transpose(1, 0, 2)
    lanes = jnp.repeat(lanes.reshape(layers, -1), vec_count, axis=1)

    half = block_size // 2
    pad = -(-row_count // 8) * 8
    work = ((pad * block_size, block_size),) + ((PANEL * pad, block_size),) * 2
    block_shape = (row_count, block_size, block_size)
    rows_shape = (row_count, vec_count, block_size)
    out_shape = (dev_count, capacity * vec_count, block_size)
    diag_own, inverse, packed, tails = call(
        functools.partial(inverse_kernel, factor),
        (),
        (diag_noise, shifts.astype(f32)),
        (
            (block_shape, f32),
            (block_shape, bf16),
            ((row_count, half, block_size), bf16),
            ((TAIL, block_size), bf16),
        ),
        work,
    )
    (near,) = communicate(geometry, 0, table, pull=(half, TAIL), own=[packed, tails])
    k_all, u, outgoing = call(
        functools.partial(factor_kernel, capacity, scale),
        (target, rank),
        (near, couplings, diag_own, vectors),
        ((block_shape, f32), (rows_shape, f32), (out_shape, bf16)),
        work,
    )
    (w,) = communicate(geometry, 1, table, push=outgoing, lanes=lanes)
    p, left, outgoing = call(
        functools.partial(left_kernel, capacity, scale),
        (target, rank),
        (w, u, inverse, couplings),
        ((rows_shape, f32), (rows_shape, bf16), (out_shape, bf16)),
    )
    near, pushed = communicate(
        geometry, 2, table, pull=(vec_count, 0), own=[left], push=outgoing, lanes=lanes
    )
    t, rest = call(
        functools.partial(middle_kernel, capacity, scale),
        (target, rank),
        (near, pushed, u, p, inverse, diag_own, couplings),
        ((rows_shape, bf16), (rows_shape, f32)),
    )
    (near,) = communicate(geometry, 3, table, pull=(vec_count, 0), own=[t])
    (result,) = call(
        functools.partial(final_kernel, capacity, scale),
        (target, rank),
        (near, rest, k_all, couplings),
        ((vectors.shape, f32),),
    )
    return result


def solution(mesh):
    return jax.shard_map(
        body,
        mesh=mesh,
        in_specs=(
            P("rows", None, None),
            P("rows", None, None, None),
            P("rows", None),
            P("rows", None),
            P("rows", None),
            P(None, "rows"),
        ),
        out_specs=P(None, "rows"),
        check_vma=False,
    )
```

time: 201 us -> 167 us (0.83)
  Pallas kernels: 46.6 us -> 154 us
  blocking collectives: 95 us -> 0 us
  waiting for transfers between devices: 35.9 us -> 0.01 us
  starting transfers between devices: 11.2 us -> 5.2 us
    pallas_call x0 -> x4, Pallas kernels: none -> 111 us  [communicate(): pl.pallas_call(functools.partial(comm_kernel, geometry, pull, push is not...]
    all_to_all x3 -> x0, blocking collectives: 95 us -> none  [exchange(): x = lax.all_to_all(x, 'rows', split_axis=0, concat_axis=0, tiled=True)]
    all_to_all x2 -> x1, waiting for transfers between devices: 35.9 us -> 0.01 us  [body(): lax.all_to_all(asked.reshape(plane, layers * capacity), 'rows', 0, 0, axi...]
    all_to_all x2 -> x1, starting transfers between devices: 11.2 us -> 5.2 us  [body(): lax.all_to_all(asked.reshape(plane, layers * capacity), 'rows', 0, 0, axi...]
    pallas_call x6 -> x5, Pallas kernels: 46.6 us -> 43 us  [call(): pl.pallas_call(kernel, out_shape=[jax.ShapeDtypeStruct(shape, dtype) for...]
    unnamed x13 -> x4, local copies, waits for them, and re-layouts: 2.47 us -> 0.01 us
  transfers between devices with their start and end apart: 2 -> 1, of which waited for: 1 -> 0; matrix products, arithmetic and copies ran while one was open for 3% -> 1% of each run, Pallas kernels for 5% -> 6%
where the time goes in v1:
time: 167 us; the launch traced here: 166 us
  Pallas kernels  154 us (92%)
  starting transfers between devices  5.2 us (3%)
  other arithmetic  3.74 us (2%)
  local copies, waits for them, and re-layouts  3.31 us (2%)
    pallas_call x4, Pallas kernels, communicate(): pl.pallas_call(functools.partial(comm_kernel, geometry, pull, push is not...  111 us
    pallas_call x5, Pallas kernels, call(): pl.pallas_call(kernel, out_shape=[jax.ShapeDtypeStruct(shape, dtype) for...  43 us
    all_to_all x1, starting transfers between devices, body(): lax.all_to_all(asked.reshape(plane, layers * capacity), 'rows', 0, 0, axi...  5.2 us
  transfers between devices with their start and end apart: 1, of which 0 were waited for; matrix products, arithmetic and copies ran while one was open for 1% of the time, Pallas kernels for 6%

profile of v1, /device:TPU:0, one launch (start us, length us, event | category | flops | bytes accessed | tf_op | source)
XLA Modules:
  0.0 166.4 jit_solution(9659399538680311738)
XLA Ops:
  0.0 0.7 add_select_fusion
  0.7 0.1 copy.20
  0.8 0.1 reshape.95.target_ref
  0.9 0.0 copy-start
  0.9 0.1 fusion
  1.0 0.1 reduce_window_sum.11
  1.0 0.2 select_reduce_fusion.1.rank_ref
  1.2 0.0 copy-start.1
  1.2 0.7 broadcast_add_fusion
  1.9 0.1 copy.21
  2.0 0.1 add.64
  2.1 0.1 select_reduce_fusion
  2.2 0.7 sub.31
  2.9 5.2 %all-to-all-start = ((s32[8,1,12]{2,1,0:T(1,128)}), s32[8,1,12]{2,1,0:T(1,128)S(1)}, u32[]{:S(2)}, u32[]{:S(2)}) async-start(s32[8,1,12]{2,1,0:T(1,128)} %bitcast), calls=%async_computation | async-start | bytes 8192 | tf_op jit(solution)/shard_map/all_to_all | solution.py:456
  8.1 1.3 convert_element_type.7.shift_ref
  9.4 9.6 %shard_map.64 = (f32[14,128,128]{2,1,0:T(8,128)}, bf16[14,128,128]{2,1,0:T(8,128)(2,1)}, bf16[14,64,128]{2,1,0:T(8,128)(2,1)}, bf16[16,128]{1,0:T(8,128)(2,1)}) custom-call(bf16[14,128,128]{2,1,0:T(8,128)(2,1)} %noise_ref.1, f32[14,128]{1,0:T(8,128)} %convert_element_type.7.shift_ref), custom_call_target="tpu_custom_call" | custom-call | tf_op jit(solution)/shard_map/pallas_call | solution.py:425
  19.0 0.0 all-to-all-done
  19.0 0.6 broadcast.112
  19.5 0.6 reduce.3
  20.2 0.7 reshape.96.refs_0_
  20.8 0.1 copy.23
  20.9 0.1 copy.24
  21.0 0.1 reshape.97
  21.1 0.1 broadcast_in_dim.20
  21.2 0.7 reshape.98.refs_1_.refs_2_
  21.9 39.5 %shard_map.65.near_ref = bf16[32,208,128]{2,1,0:T(8,128)(2,1)} custom-call(s32[96]{0:T(128)} %reshape.96.refs_0_, bf16[14,64,128]{2,1,0:T(8,128)(2,1)} %get-tuple-element.19.refs_1_, bf16[16,128]{1,0:T(8,128)(2,1)} %get-tuple-element.20.refs_2_), custom_call_target="tpu_custom_call" | custom-call | tf_op jit(solution)/shard_map/pallas_call | solution.py:412
  61.4 0.0 copy-done
  61.4 0.0 copy-done.1
  61.4 18.2 %shard_map.66 = (f32[14,128,128]{2,1,0:T(8,128)}, f32[14,32,128]{2,1,0:T(8,128)}, bf16[32,96,128]{2,1,0:T(8,128)(2,1)}) custom-call(s32[42]{0:T(128)} %copy-done, s32[42]{0:T(128)} %copy-done.1, bf16[32,208,128]{2,1,0:T(8,128)(2,1)} %shard_map.65.near_ref, bf16[14,3,128,128]{3,2,1,0:T(8,128)(2,1)} %c_ref.7, f32[14,128,128]{2,1,0:T(8,128)} %get-tuple-element.21.d_ref, ...), custom_call_target="tpu_custom_call" | custom-call | tf_op jit(solution)/shard_map/pallas_call | solution.py:425
  79.6 22.1 %shard_map.67.w_ref = f32[448,128]{1,0:T(8,128)} custom-call(s32[96]{0:T(128)} %reshape.96.refs_0_, s32[4,768]{1,0:T(4,128)} %reshape.98.refs_1_.refs_2_, bf16[32,96,128]{2,1,0:T(8,128)(2,1)} %get-tuple-element.22.refs_2_), custom_call_target="tpu_custom_call" | custom-call | tf_op jit(solution)/shard_map/pallas_call | solution.py:412
  101.8 4.7 %shard_map.68 = (f32[14,32,128]{2,1,0:T(8,128)}, bf16[14,32,128]{2,1,0:T(8,128)(2,1)}, bf16[32,96,128]{2,1,0:T(8,128)(2,1)}) custom-call(s32[42]{0:T(128)} %copy-done, s32[42]{0:T(128)} %copy-done.1, f32[448,128]{1,0:T(8,128)} %shard_map.67.w_ref, f32[14,32,128]{2,1,0:T(8,128)} %get-tuple-element.23.u_ref, bf16[14,128,128]{2,1,0:T(8,128)(2,1)} %get-tuple-element.24.e_ref, ...), custom_call_target="tpu_custom_call" | custom-call | tf_op jit(solution)/shard_map/pallas_call | solution.py:425
  106.4 25.3 %shard_map.69 = (bf16[32,96,128]{2,1,0:T(8,128)(2,1)}, f32[448,128]{1,0:T(8,128)}) custom-call(s32[96]{0:T(128)} %reshape.96.refs_0_, bf16[14,32,128]{2,1,0:T(8,128)(2,1)} %get-tuple-element.25.refs_1_, s32[4,768]{1,0:T(4,128)} %reshape.98.refs_1_.refs_2_, bf16[32,96,128]{2,1,0:T(8,128)(2,1)} %get-tuple-element.26.refs_3_), custom_call_target="tpu_custom_call" | custom-call | tf_op jit(solution)/shard_map/pallas_call | solution.py:412
  131.7 5.6 %shard_map.70 = (bf16[14,32,128]{2,1,0:T(8,128)(2,1)}, f32[14,32,128]{2,1,0:T(8,128)}) custom-call(s32[42]{0:T(128)} %copy-done, s32[42]{0:T(128)} %copy-done.1, bf16[32,96,128]{2,1,0:T(8,128)(2,1)} %get-tuple-element.27.near_ref, f32[448,128]{1,0:T(8,128)} %get-tuple-element.28.pushed_ref, f32[14,32,128]{2,1,0:T(8,128)} %get-tuple-element.23.u_ref, ...), custom_call_target="tpu_custom_call" | custom-call | tf_op jit(solution)/shard_map/pallas_call | solution.py:425
  137.3 24.1 %shard_map.71.near_ref = bf16[32,96,128]{2,1,0:T(8,128)(2,1)} custom-call(s32[96]{0:T(128)} %reshape.96.refs_0_, bf16[14,32,128]{2,1,0:T(8,128)(2,1)} %get-tuple-element.30.refs_1_), custom_call_target="tpu_custom_call" | custom-call | tf_op jit(solution)/shard_map/pallas_call | solution.py:412
  161.4 5.0 %shard_map.72 = f32[32,1792]{1,0:T(8,128)} custom-call(s32[42]{0:T(128)} %copy-done, s32[42]{0:T(128)} %copy-done.1, bf16[32,96,128]{2,1,0:T(8,128)(2,1)} %shard_map.71.near_ref, f32[14,32,128]{2,1,0:T(8,128)} %get-tuple-element.31.rest_ref, f32[14,128,128]{2,1,0:T(8,128)} %get-tuple-element.32.k_ref, bf16[14,3,128,128]{3,2,1,0:T(8,128)(2,1)} %c_ref.7), custom_call_target="tpu_custom_call" | custom-call | tf_op jit(solution)/shard_map/pallas_call | solution.py:425
  (3 shorter events, 0.0 us)
Async XLA Ops:
  0.9 60.5 %copy-start = (s32[42]{0:T(128)}, s32[42]{0:T(128)S(1)}, u32[]{:S(2)}) copy-start(s32[42]{0:T(128)S(1)} %reshape.95.target_ref) | copy-start | bytes 508
  1.2 60.2 %copy-start.1 = (s32[42]{0:T(128)}, s32[42]{0:T(128)S(1)}, u32[]{:S(2)}) copy-start(s32[42]{0:T(128)S(1)} %select_reduce_fusion.1.rank_ref) | copy-start | bytes 508
  2.9 16.1 %all-to-all-start = ((s32[8,1,12]{2,1,0:T(1,128)}), s32[8,1,12]{2,1,0:T(1,128)S(1)}, u32[]{:S(2)}, u32[]{:S(2)}) async-start(s32[8,1,12]{2,1,0:T(1,128)} %bitcast), calls=%async_computation | async-start | bytes 8192 | tf_op jit(solution)/shard_map/all_to_all | solution.py:456

commit v2 on v1

--- a/solution.py
+++ b/solution.py
@@ -242,7 +242,7 @@
     if push:
         (sum_ref,) = take(1)
     if pull:
-        zbuf = [take(parts) for _ in range(layers - 1)]
+        relayed = {(d, s): take(parts) for d in (-1, 1) for s in range(layers - 1)}
         (send_ref,) = take(1)
     if push:
         arrive_ref, zout_ref, zin_ref = take(3)
@@ -270,42 +270,74 @@
 
     if pull:
         tail_row = lax.broadcasted_iota(jnp.int32, (TAIL, 128), 0)
-        pull_z = [
-            [
+
+        def held(d, s):
+            return own_ref if s < 0 else relayed[d, s]
+
+        def hop(d, s):
+            side = 0 if d < 0 else 1
+            there = jnp.clip(z - d, 0, layers - 1)
+            return [
                 remote(
-                    own_ref[i], zbuf[o - 1][i], pz_send.at[o - 1, i], pz_recv.at[o - 1, i],
-                    zs[o] * plane + q,
+                    held(d, s - 1)[i], relayed[d, s][i], pz_send.at[side, s, i],
+                    pz_recv.at[side, s, i], there * plane + q,
                 )
                 for i in range(parts)
             ]
-            for o in range(1, layers)
-        ]
-        pull_p = {
-            (o, e): remote(
-                send_ref.at[o * plane + e], near_ref.at[zs[o] * plane + q],
-                pp_send.at[o, e], pp_recv.at[o, e], z * plane + qs[e],
+
+        def inside(x):
+            return (x >= 0) & (x < layers)
+
+        def spread(d, s, e):
+            layer = z if s < 0 else jnp.clip(z + d * (s + 1), 0, layers - 1)
+            return remote(
+                send_ref.at[layer, e], near_ref.at[layer * plane + q],
+                pp_send.at[layer, e], pp_recv.at[layer, e], z * plane + qs[e],
             )
-            for o in range(layers)
-            for e in range(1, plane)
-        }
-
-        def pack(o, e):
-            source = own_ref if o == 0 else zbuf[o - 1]
-            target, slot = (near_ref, zs[o] * plane + q) if e == 0 else (send_ref, o * plane + e)
+
+        def pack(d, s, e):
+            source = held(d, s)
+            layer = z if s < 0 else jnp.clip(z + d * (s + 1), 0, layers - 1)
             tile = jnp.zeros((TAIL, 128), f32)
             if tail:
                 every = source[1][...].astype(f32)
+
+            def put(rows, value):
+                if e == 0:
+                    near_ref[layer * plane + q, rows, :] = value
+                else:
+                    send_ref[layer, e, rows, :] = value
+
             for c in range(capacity):
-                index = jnp.maximum(table_ref[(qs[e] * layers + zs[o]) * capacity + c], 0)
-                target[slot, pl.ds(c * height, height), :] = source[0][index]
+                index = jnp.maximum(table_ref[(qs[e] * layers + layer) * capacity + c], 0)
+                put(pl.ds(c * height, height), source[0][index])
                 if tail:
                     line = jnp.sum(jnp.where(tail_row == index, every, 0.0), axis=0, keepdims=True)
                     tile = jnp.where(tail_row == c, line, tile)
             if tail:
-                target[slot, pl.ds(capacity * height, TAIL), :] = tile.astype(bf16)
-
-        for e in range(1, plane):
-            pack(0, e)
+                put(pl.ds(capacity * height, TAIL), tile.astype(bf16))
+
+        def serve(d, s):
+            for e in reversed(range(plane)):
+                pack(d, s, e)
+                if e:
+                    spread(d, s, e).start()
+
+        def advance(d, s):
+            @pl.when(inside(z + d * (s + 1)))
+            def _():
+                for copy in hop(d, s):
+                    copy.wait_recv()
+            if s < layers - 2:
+                @pl.when(inside(z + d * (s + 1)) & inside(z - d))
+                def _():
+                    for copy in hop(d, s + 1):
+                        copy.start()
+
+            @pl.when(inside(z + d * (s + 1)))
+            def _():
+                serve(d, s)
+
     if push:
         step = out_ref.shape[1]
         vec = step // capacity
@@ -333,40 +365,38 @@
             )
             return dot_nn(pick, arrive_ref[zs[o]])
 
+    far_first = list(reversed(range(1, layers)))
     pl.semaphore_wait(barrier, len(partners))
     if pull:
-        for o in reversed(range(1, layers)):
-            for copy in pull_z[o - 1]:
-                copy.start()
-    if push:
-        for o in list(range(1, layers)) + [0]:
+        for d in (-1, 1):
+            @pl.when(inside(z - d))
+            def _():
+                for copy in hop(d, 0):
+                    copy.start()
+    if push:
+        for o in far_first + [0]:
             for e in reversed(range(1, plane)):
                 push_p[o, e].start()
+    if pull:
+        serve(0, -1)
+    if push:
         for o in range(layers):
             here = pl.ds(pl.multiple_of(q * step, step), step)
             arrive_ref[zs[o], here, :] = out_ref[zs[o] * plane + q]
-    if pull:
-        for e in reversed(range(1, plane)):
-            pull_p[0, e].start()
-        pack(0, 0)
-    for o in range(1, layers):
+    for i, o in enumerate(far_first):
         if push:
             for e in range(1, plane):
                 push_p[o, e].wait_recv()
             zout_ref[o - 1] = gather_sum(o).astype(bf16)
             push_z[o - 1].start()
         if pull:
-            for copy in pull_z[o - 1]:
-                copy.wait_recv()
-            for e in reversed(range(1, plane)):
-                pack(o, e)
-                pull_p[o, e].start()
-            pack(o, 0)
+            advance(-1, i)
+            advance(1, i)
     if push:
         for e in range(1, plane):
             push_p[0, e].wait_recv()
         total_sum = gather_sum(0)
-        for o in range(1, layers):
+        for o in far_first:
             push_z[o - 1].wait_recv()
             total_sum = total_sum + zin_ref[o - 1].astype(f32)
         sum_ref[...] = total_sum
@@ -375,12 +405,19 @@
         for copy in push_p.values():
             copy.wait_send()
     if pull:
-        for copy in pull_p.values():
-            copy.wait_recv()
-        for copy in pull_p.values():
-            copy.wait_send()
-        for copies in pull_z:
-            for copy in copies:
+        for d in (-1, 1):
+            for s in range(layers - 1):
+                @pl.when(inside(z - d) & inside(z + d * s))
+                def _():
+                    for copy in hop(d, s):
+                        copy.wait_send()
+        for layer in range(layers):
+            for e in range(1, plane):
+                copy = remote(
+                    send_ref.at[layer, e], near_ref.at[layer * plane + q],
+                    pp_send.at[layer, e], pp_recv.at[layer, e], z * plane + qs[e],
+                )
+                copy.wait_recv()
                 copy.wait_send()
 
 
@@ -397,9 +434,9 @@
         height, tail = pull
         block = (capacity * height + tail, own[0].shape[-1])
         shapes += [jax.ShapeDtypeStruct((total,) + block, bf16)]
-        scratch += [pltpu.VMEM(part.shape, bf16) for part in own] * (layers - 1)
-        scratch += [pltpu.VMEM((total,) + block, bf16)]
-        sems += [dma((layers - 1, len(own)))] * 2 + [dma((layers, plane))] * 2
+        scratch += [pltpu.VMEM(part.shape, bf16) for part in own] * (2 * layers - 2)
+        scratch += [pltpu.VMEM((layers, plane) + block, bf16)]
+        sems += [dma((2, layers - 1, len(own)))] * 2 + [dma((layers, plane))] * 2
     if push is not None:
         args += [lanes, push]
         specs += [vmem, vmem]

time: 167 us -> 159 us (0.952)
  Pallas kernels: 154 us -> 146 us
    pallas_call x4, Pallas kernels: 111 us -> 103 us  [communicate(): pl.pallas_call(functools.partial(comm_kernel, geometry, pull, push is not...]
where the time goes in v2:
time: 159 us; the launch traced here: 158 us
  Pallas kernels  146 us (92%)
  starting transfers between devices  5.2 us (3%)
  other arithmetic  3.74 us (2%)
  local copies, waits for them, and re-layouts  3.31 us (2%)
    pallas_call x4, Pallas kernels, communicate(): pl.pallas_call(functools.partial(comm_kernel, geometry, pull, push is not...  103 us
    pallas_call x5, Pallas kernels, call(): pl.pallas_call(kernel, out_shape=[jax.ShapeDtypeStruct(shape, dtype) for...  43 us
    all_to_all x1, starting transfers between devices, body(): lax.all_to_all(asked.reshape(plane, layers * capacity), 'rows', 0, 0, axi...  5.2 us
  transfers between devices with their start and end apart: 1, of which 0 were waited for; matrix products, arithmetic and copies ran while one was open for 1% of the time, Pallas kernels for 6%

profile of v2, /device:TPU:0, one launch (start us, length us, event | category | flops | bytes accessed | tf_op | source)
XLA Modules:
  0.0 158.5 jit_solution(17588018542479793382)
XLA Ops:
  0.0 0.7 add_select_fusion
  0.7 0.1 copy.20
  0.8 0.1 reshape.95.target_ref
  0.9 0.0 copy-start
  0.9 0.1 fusion
  1.0 0.1 reduce_window_sum.11
  1.0 0.2 select_reduce_fusion.1.rank_ref
  1.2 0.0 copy-start.1
  1.2 0.7 broadcast_add_fusion
  1.9 0.1 copy.21
  2.0 0.1 add.64
  2.1 0.1 select_reduce_fusion
  2.2 0.7 sub.31
  2.9 5.2 %all-to-all-start = ((s32[8,1,12]{2,1,0:T(1,128)}), s32[8,1,12]{2,1,0:T(1,128)S(1)}, u32[]{:S(2)}, u32[]{:S(2)}) async-start(s32[8,1,12]{2,1,0:T(1,128)} %bitcast), calls=%async_computation | async-start | bytes 8192 | tf_op jit(solution)/shard_map/all_to_all | solution.py:493
  8.1 1.3 convert_element_type.7.shift_ref
  9.4 9.6 %shard_map.64 = (f32[14,128,128]{2,1,0:T(8,128)}, bf16[14,128,128]{2,1,0:T(8,128)(2,1)}, bf16[14,64,128]{2,1,0:T(8,128)(2,1)}, bf16[16,128]{1,0:T(8,128)(2,1)}) custom-call(bf16[14,128,128]{2,1,0:T(8,128)(2,1)} %noise_ref.1, f32[14,128]{1,0:T(8,128)} %convert_element_type.7.shift_ref), custom_call_target="tpu_custom_call" | custom-call | tf_op jit(solution)/shard_map/pallas_call | solution.py:462
  19.0 0.0 all-to-all-done
  19.0 0.6 broadcast.112
  19.5 0.6 reduce.3
  20.2 0.7 reshape.96.refs_0_
  20.8 0.1 copy.23
  20.9 0.1 copy.24
  21.0 0.1 reshape.97
  21.1 0.1 broadcast_in_dim.20
  21.2 0.7 reshape.98.refs_1_.refs_2_
  21.9 31.3 %shard_map.65.near_ref = bf16[32,208,128]{2,1,0:T(8,128)(2,1)} custom-call(s32[96]{0:T(128)} %reshape.96.refs_0_, bf16[14,64,128]{2,1,0:T(8,128)(2,1)} %get-tuple-element.19.refs_1_, bf16[16,128]{1,0:T(8,128)(2,1)} %get-tuple-element.20.refs_2_), custom_call_target="tpu_custom_call" | custom-call | tf_op jit(solution)/shard_map/pallas_call | solution.py:449
  53.1 0.0 copy-done
  53.1 0.0 copy-done.1
  53.2 18.2 %shard_map.66 = (f32[14,128,128]{2,1,0:T(8,128)}, f32[14,32,128]{2,1,0:T(8,128)}, bf16[32,96,128]{2,1,0:T(8,128)(2,1)}) custom-call(s32[42]{0:T(128)} %copy-done, s32[42]{0:T(128)} %copy-done.1, bf16[32,208,128]{2,1,0:T(8,128)(2,1)} %shard_map.65.near_ref, bf16[14,3,128,128]{3,2,1,0:T(8,128)(2,1)} %c_ref.7, f32[14,128,128]{2,1,0:T(8,128)} %get-tuple-element.21.d_ref, ...), custom_call_target="tpu_custom_call" | custom-call | tf_op jit(solution)/shard_map/pallas_call | solution.py:462
  71.4 21.4 %shard_map.67.w_ref = f32[448,128]{1,0:T(8,128)} custom-call(s32[96]{0:T(128)} %reshape.96.refs_0_, s32[4,768]{1,0:T(4,128)} %reshape.98.refs_1_.refs_2_, bf16[32,96,128]{2,1,0:T(8,128)(2,1)} %get-tuple-element.22.refs_2_), custom_call_target="tpu_custom_call" | custom-call | tf_op jit(solution)/shard_map/pallas_call | solution.py:449
  92.8 4.7 %shard_map.68 = (f32[14,32,128]{2,1,0:T(8,128)}, bf16[14,32,128]{2,1,0:T(8,128)(2,1)}, bf16[32,96,128]{2,1,0:T(8,128)(2,1)}) custom-call(s32[42]{0:T(128)} %copy-done, s32[42]{0:T(128)} %copy-done.1, f32[448,128]{1,0:T(8,128)} %shard_map.67.w_ref, f32[14,32,128]{2,1,0:T(8,128)} %get-tuple-element.23.u_ref, bf16[14,128,128]{2,1,0:T(8,128)(2,1)} %get-tuple-element.24.e_ref, ...), custom_call_target="tpu_custom_call" | custom-call | tf_op jit(solution)/shard_map/pallas_call | solution.py:462
  97.5 31.0 %shard_map.69 = (bf16[32,96,128]{2,1,0:T(8,128)(2,1)}, f32[448,128]{1,0:T(8,128)}) custom-call(s32[96]{0:T(128)} %reshape.96.refs_0_, bf16[14,32,128]{2,1,0:T(8,128)(2,1)} %get-tuple-element.25.refs_1_, s32[4,768]{1,0:T(4,128)} %reshape.98.refs_1_.refs_2_, bf16[32,96,128]{2,1,0:T(8,128)(2,1)} %get-tuple-element.26.refs_3_), custom_call_target="tpu_custom_call" | custom-call | tf_op jit(solution)/shard_map/pallas_call | solution.py:449
  128.5 5.6 %shard_map.70 = (bf16[14,32,128]{2,1,0:T(8,128)(2,1)}, f32[14,32,128]{2,1,0:T(8,128)}) custom-call(s32[42]{0:T(128)} %copy-done, s32[42]{0:T(128)} %copy-done.1, bf16[32,96,128]{2,1,0:T(8,128)(2,1)} %get-tuple-element.27.near_ref, f32[448,128]{1,0:T(8,128)} %get-tuple-element.28.pushed_ref, f32[14,32,128]{2,1,0:T(8,128)} %get-tuple-element.23.u_ref, ...), custom_call_target="tpu_custom_call" | custom-call | tf_op jit(solution)/shard_map/pallas_call | solution.py:462
  134.1 19.3 %shard_map.71.near_ref = bf16[32,96,128]{2,1,0:T(8,128)(2,1)} custom-call(s32[96]{0:T(128)} %reshape.96.refs_0_, bf16[14,32,128]{2,1,0:T(8,128)(2,1)} %get-tuple-element.30.refs_1_), custom_call_target="tpu_custom_call" | custom-call | tf_op jit(solution)/shard_map/pallas_call | solution.py:449
  153.5 5.0 %shard_map.72 = f32[32,1792]{1,0:T(8,128)} custom-call(s32[42]{0:T(128)} %copy-done, s32[42]{0:T(128)} %copy-done.1, bf16[32,96,128]{2,1,0:T(8,128)(2,1)} %shard_map.71.near_ref, f32[14,32,128]{2,1,0:T(8,128)} %get-tuple-element.31.rest_ref, f32[14,128,128]{2,1,0:T(8,128)} %get-tuple-element.32.k_ref, bf16[14,3,128,128]{3,2,1,0:T(8,128)(2,1)} %c_ref.7), custom_call_target="tpu_custom_call" | custom-call | tf_op jit(solution)/shard_map/pallas_call | solution.py:462
  (3 shorter events, 0.0 us)
Async XLA Ops:
  0.9 52.3 %copy-start = (s32[42]{0:T(128)}, s32[42]{0:T(128)S(1)}, u32[]{:S(2)}) copy-start(s32[42]{0:T(128)S(1)} %reshape.95.target_ref) | copy-start | bytes 508
  1.2 51.9 %copy-start.1 = (s32[42]{0:T(128)}, s32[42]{0:T(128)S(1)}, u32[]{:S(2)}) copy-start(s32[42]{0:T(128)S(1)} %select_reduce_fusion.1.rank_ref) | copy-start | bytes 508
  2.9 16.1 %all-to-all-start = ((s32[8,1,12]{2,1,0:T(1,128)}), s32[8,1,12]{2,1,0:T(1,128)S(1)}, u32[]{:S(2)}, u32[]{:S(2)}) async-start(s32[8,1,12]{2,1,0:T(1,128)} %bitcast), calls=%async_computation | async-start | bytes 8192 | tf_op jit(solution)/shard_map/all_to_all | solution.py:493

commit v3 on v0

v3 whole, which is shorter than its diff:
```python
import functools
import math

import jax
import jax.numpy as jnp
from jax import lax
from jax.experimental import pallas as pl
from jax.experimental.pallas import tpu as pltpu
from jax.sharding import PartitionSpec as P

PANEL = 16
GROUP = 4
LAYERS = 4
TAIL = 16
UNROLL = 7
MESH = pl.DeviceIdType.MESH
bf16, f32 = jnp.bfloat16, jnp.float32


def split2(x):
    high = x.astype(bf16)
    return high, (x - high.astype(f32)).astype(bf16)


def joined(*parts):
    return jnp.concatenate(parts, axis=-1)


def tdot(a, b):
    return lax.dot_general(a, b, (((0,), (0,)), ((), ())), preferred_element_type=f32)


def dot_nn(a, b):
    return jnp.dot(a, b, preferred_element_type=f32)


def dot_nt(a, b):
    return lax.dot_general(a, b, (((1,), (1,)), ((), ())), preferred_element_type=f32)


def eliminate(m, pscr, qscr, count, pad, size):
    panel = PANEL
    lane = lax.broadcasted_iota(jnp.int32, (pad, size), 1)
    for block in reversed(range(size // panel)):
        base = block * panel
        rows = [m[pl.ds(base + r, pad, stride=size), :] for r in range(panel)]
        for k in reversed(range(panel)):
            col = base + k
            here = lane == col
            if (k + 1) % GROUP == 0:
                first = k + 1 - GROUP
                tile = {
                    (i, c): jnp.broadcast_to(rows[i][:, base + c : base + c + 1], (pad, size))
                    for c in range(first, k + 1)
                    for i in range(c + 1)
                }
            inv = 1.0 / tile[k, k]
            for c in reversed(range(first, k)):
                ratio = tile[c, k] * inv
                for i in range(c + 1):
                    tile[i, c] = tile[i, c] - tile[i, k] * ratio
            pivot_row = jnp.where(here, 1.0, rows[k])
            scaled = pivot_row * inv
            for i in range(k):
                rows[i] = jnp.where(here, 0.0, rows[i]) - tile[i, k] * scaled
            if block:
                pscr[pl.ds(k * pad, pad), :] = jnp.where(
                    (lane >= base) & (lane < col), 0.0, pivot_row
                )
                qscr[pl.ds(k * pad, pad), :] = scaled
            m[pl.ds(col, pad, stride=size), :] = jnp.where(
                lane >= col, pivot_row * jnp.sqrt(inv), 0.0
            )
        if block:
            lane_m = lax.broadcasted_iota(jnp.int32, (base, size), 1)
            inside = (lane_m >= base) & (lane_m < base + panel)
            for n in range(count):
                ph, plow = split2(pscr[pl.ds(n, panel, stride=pad), :])
                qh, qlow = split2(qscr[pl.ds(n, panel, stride=pad), :])
                right = jnp.concatenate([ph, plow, ph], axis=0)
                left = jnp.concatenate([qh, qh, qlow], axis=0)
                update = tdot(left, right)[:base]
                spot = pl.ds(n * size, base)
                m[spot, :] = jnp.where(inside, 0.0, m[spot, :]) - update


def inside(x, layers):
    return (x >= 0) & (x < layers)


class Links:
    def __init__(self, total, layers):
        self.layers, self.plane = layers, total // layers
        me = lax.axis_index("rows")
        self.z = me // self.plane
        self.q = lax.rem(me, self.plane)
        self.zs = [jnp.bitwise_xor(self.z, o) for o in range(layers)]
        self.qs = [jnp.bitwise_xor(self.q, e) for e in range(self.plane)]

    def partners(self):
        far = [self.zs[o] * self.plane + self.q for o in range(1, self.layers)]
        return far + [self.z * self.plane + self.qs[e] for e in range(1, self.plane)]

    def remote(self, src, dst, send, recv, device):
        return pltpu.make_async_remote_copy(
            src_ref=src, dst_ref=dst, send_sem=send, recv_sem=recv,
            device_id=(device,), device_id_type=MESH,
        )


class Pull:
    def __init__(self, links, table_ref, capacity, count, tail, refs):
        self.links, self.table, self.capacity, self.tail = links, table_ref, capacity, tail
        self.own, self.send, self.near, *rest = refs
        moves = [(d, s) for s in range(links.layers - 1) for d in (-1, 1)]
        self.relayed = dict(zip(moves, rest))
        self.z_send, self.z_recv, self.p_send, self.p_recv = rest[len(moves):]
        self.tiles = (self.own.shape[0] - tail) // count
        self.last = count * self.tiles
        self.group = capacity * self.tiles + tail

    def held(self, d, s):
        return self.own if s < 0 else self.relayed[d, s]

    def layer(self, d, s):
        return self.links.z if s < 0 else jnp.clip(self.links.z + d * (s + 1), 0, self.links.layers - 1)

    def hop(self, d, s):
        k = self.links
        side = 0 if d < 0 else 1
        there = jnp.clip(k.z - d, 0, k.layers - 1)
        return k.remote(
            self.held(d, s - 1), self.relayed[d, s], self.z_send.at[side, s],
            self.z_recv.at[side, s], there * k.plane + k.q,
        )

    def spread(self, layer, e):
        k = self.links
        return k.remote(
            self.send.at[layer, e], self.near.at[layer * k.plane + k.q],
            self.p_send.at[layer, e], self.p_recv.at[layer, e], k.z * k.plane + k.qs[e],
        )

    def pack(self, d, s, e):
        k = self.links
        source, layer = self.held(d, s), self.layer(d, s)

        def put(spot, value):
            if e == 0:
                self.near[layer * k.plane + k.q, spot] = value
            else:
                self.send[layer, e, spot] = value

        if self.tail:
            row = lax.broadcasted_iota(jnp.int32, (TAIL, 128), 0)
            tile = jnp.zeros((TAIL, 128), f32)
            every = source[self.last].astype(f32)
        for c in range(self.capacity):
            index = jnp.maximum(self.table[(k.qs[e] * k.layers + layer) * self.capacity + c], 0)
            for i in range(self.tiles):
                put(c * self.tiles + i, source[index * self.tiles + i])
            if self.tail:
                line = jnp.sum(jnp.where(row == index, every, 0.0), axis=0, keepdims=True)
                tile = jnp.where(row == c, line, tile)
        if self.tail:
            put(self.capacity * self.tiles, tile.astype(bf16))

    def serve(self, d, s):
        for e in reversed(range(self.links.plane)):
            self.pack(d, s, e)
            if e:
                self.spread(self.layer(d, s), e).start()

    def start(self):
        for d in (-1, 1):
            @pl.when(inside(self.links.z - d, self.links.layers))
            def _():
                self.hop(d, 0).start()

    def advance(self, d, s):
        z, layers = self.links.z, self.links.layers

        @pl.when(inside(z + d * (s + 1), layers))
        def _():
            self.hop(d, s).wait_recv()
        if s < layers - 2:
            @pl.when(inside(z + d * (s + 1), layers) & inside(z - d, layers))
            def _():
                self.hop(d, s + 1).start()

        @pl.when(inside(z + d * (s + 1), layers))
        def _():
            self.serve(d, s)

    def finish(self):
        z, layers = self.links.z, self.links.layers
        for d in (-1, 1):
            for s in range(layers - 1):
                @pl.when(inside(z - d, layers) & inside(z + d * s, layers))
                def _():
                    self.hop(d, s).wait_send()
        for layer in range(layers):
            for e in range(1, self.links.plane):
                self.spread(layer, e).wait_recv()
                self.spread(layer, e).wait_send()


class Push:
    def __init__(self, links, slot_ref, lanes_ref, capacity, count, refs):
        self.links, self.slot, self.lanes, self.capacity, self.count = (
            links, slot_ref, lanes_ref, capacity, count,
        )
        self.given, self.out, self.arrive, self.zout, self.zin, *sems = refs
        self.z_send, self.z_recv, self.p_send, self.p_recv = sems
        self.group = self.out.shape[1]
        self.tiles = self.group // capacity

    def spread(self, o, e):
        k = self.links
        here = pl.ds(pl.multiple_of(k.q * self.group, self.group), self.group)
        return k.remote(
            self.out.at[k.zs[o] * k.plane + k.qs[e]], self.arrive.at[k.zs[o], here],
            self.p_send.at[o, e], self.p_recv.at[o, e], k.z * k.plane + k.qs[e],
        )

    def hop(self, o):
        k = self.links
        return k.remote(
            self.zout.at[o - 1], self.zin.at[o - 1], self.z_send.at[o - 1],
            self.z_recv.at[o - 1], k.zs[o] * k.plane + k.q,
        )

    def order(self):
        return list(reversed(range(1, self.links.layers)))

    def serve(self, o):
        k = self.links
        for e in reversed(range(k.plane)):
            device = k.zs[o] * k.plane + k.qs[e]
            for c in range(self.capacity):
                index = jnp.maximum(self.slot[device * self.capacity + c], 0)
                for i in range(self.tiles):
                    value = self.given[index * self.tiles + i]
                    if e:
                        self.out[device, c * self.tiles + i] = value
                    else:
                        self.arrive[k.zs[o], k.q * self.group + c * self.tiles + i] = value
            if e:
                self.spread(o, e).start()

    def gathered(self, o):
        k = self.links
        for e in range(1, k.plane):
            self.spread(o, e).wait_recv()
        arrived = self.arrive[k.zs[o]]
        arrived = arrived.reshape(-1, arrived.shape[-1])
        vec = self.tiles * arrived.shape[0] // (k.plane * self.group)
        lanes = self.lanes[pl.ds(k.zs[o], 1), :]
        shape = (vec, arrived.shape[0])
        row = lax.broadcasted_iota(jnp.int32, shape, 0)
        col = lax.broadcasted_iota(jnp.int32, shape, 1)
        same = row == lax.rem(col, vec)
        pick = [jnp.where(same & (lanes == i), 1.0, 0.0).astype(bf16) for i in range(self.count)]
        return dot_nn(jnp.concatenate(pick, axis=0), arrived)

    def advance(self, o):
        self.zout[o - 1] = self.gathered(o).astype(bf16)
        self.hop(o).start()

    def finish(self):
        total = self.gathered(0)
        for o in self.order():
            self.hop(o).wait_recv()
            total = total + self.zin[o - 1].astype(f32)
        for o in range(self.links.layers):
            if o:
                self.hop(o).wait_send()
            for e in range(1, self.links.plane):
                self.spread(o, e).wait_send()
        return total


def whole_kernel(
    geometry, factor, scale, counts,
    table_ref, slot_ref, target_ref, rank_ref, lanes_ref, noise_ref, shift_ref, c_ref, v_ref,
    result_ref, *scratch,
):
    total, layers, capacity = geometry
    count, size, _ = noise_ref.shape
    vec = v_ref.shape[0]
    half = size // 2
    scratch = list(scratch)
    take = lambda k: [scratch.pop(0) for _ in range(k)]
    d_ref, e_ref, u_ref, p_ref, rest_ref, m, pscr, qscr = take(8)
    pad = m.shape[0] // size
    links = Links(total, layers)
    pull_e = Pull(links, table_ref, capacity, count, 1, take(counts[0]))
    pull_left = Pull(links, table_ref, capacity, count, 0, take(counts[0]))
    pull_t = Pull(links, table_ref, capacity, count, 0, take(counts[0]))
    push_w = Push(links, slot_ref, lanes_ref, capacity, count, take(counts[1]))
    push_p = Push(links, slot_ref, lanes_ref, capacity, count, take(counts[1]))

    barrier = pltpu.get_barrier_semaphore()
    for device in links.partners():
        pl.semaphore_signal(barrier, inc=1, device_id=(device,), device_id_type=MESH)

    row_full = lax.broadcasted_iota(jnp.int32, (size, size), 0)
    col_full = lax.broadcasted_iota(jnp.int32, (size, size), 1)
    on_diag = row_full == col_full
    for n in range(count):
        noise = noise_ref[n].astype(f32)
        d = (noise + noise.T) * (0.5 * factor)
        d = d + jnp.where(on_diag, shift_ref[pl.ds(n, 1), :], 0.0)
        d_ref[n] = d
        m[pl.ds(n * size, size), :] = d
        if n < pad - count:
            m[pl.ds((count + n) * size, size), :] = d
    eliminate(m, pscr, qscr, count, pad, size)
    row = lax.broadcasted_iota(jnp.int32, (half, half), 0)
    col = lax.broadcasted_iota(jnp.int32, (half, half), 1)
    tail_row = lax.broadcasted_iota(jnp.int32, (TAIL, size), 0)
    tile = jnp.zeros((TAIL, size), f32)
    parts = half // TAIL
    for n in range(count):
        h, low = split2(m[pl.ds(n * size, size), :])
        e = tdot(jnp.concatenate([h, h, low], axis=0), jnp.concatenate([h, low, h], axis=0))
        e_ref[n] = e.astype(bf16)
        left = jnp.where(row >= col, e[:half, :half], e[half:, half:])
        packed = joined(left, e[:half, half:]).astype(bf16)
        for i in range(parts):
            pull_e.own[n * parts + i] = packed[i * TAIL : (i + 1) * TAIL]
        diag = jnp.sum(jnp.where(on_diag, e, 0.0), axis=0, keepdims=True)
        tile = jnp.where(tail_row == n, diag, tile)
    pull_e.own[count * parts] = tile.astype(bf16)

    pl.semaphore_wait(barrier, len(links.partners()))
    pull_e.start()
    pull_e.serve(0, -1)
    for s in range(layers - 1):
        pull_e.advance(-1, s)
        pull_e.advance(1, s)
    pull_e.finish()

    def schur(n, carry):
        fs, cs = [], []
        for k in range(3):
            t = target_ref[3 * n + k]
            c = rank_ref[3 * n + k]
            packed = jnp.concatenate(
                [pull_e.near[t, c * parts + i] for i in range(parts)], axis=0
            ).astype(f32)
            tile = pull_e.near[t, capacity * parts].astype(f32)
            diag = jnp.sum(jnp.where(tail_row == c, tile, 0.0), axis=0, keepdims=True)
            flipped = packed.T
            part = packed[:, :half]
            part_t = flipped[:half, :]
            first = jnp.where(row >= col, part, part_t)
            last = jnp.where(row < col, part, part_t)
            last = jnp.where(row == col, diag[:, half:], last)
            inverse = jnp.concatenate(
                [joined(first, packed[:, half:]), joined(flipped[half:, :], last)], axis=0
            ).astype(bf16)
            coupling = c_ref[n, k]
            fs.append((dot_nn(coupling, inverse) * (scale * scale)).astype(bf16))
            cs.append(coupling)
        reduced = d_ref[n] - dot_nt(joined(*fs), joined(*cs))
        m[pl.ds(pl.multiple_of(n * size, size), size), :] = reduced
        return carry

    lax.fori_loop(0, count, schur, 0, unroll=UNROLL)
    for n in range(count, pad):
        m[pl.ds(n * size, size), :] = d_ref[0]
    eliminate(m, pscr, qscr, count, pad, size)

    def give(push, n, x):
        low = (x * scale).astype(bf16)
        for k in range(3):
            value = dot_nn(low, c_ref[n, k]).astype(bf16)
            for i in range(vec // TAIL):
                push.given[(3 * n + k) * (vec // TAIL) + i] = value[i * TAIL : (i + 1) * TAIL]

    def offer(pull, n, x):
        for i in range(vec // TAIL):
            pull.own[n * (vec // TAIL) + i] = x[i * TAIL : (i + 1) * TAIL].astype(bf16)

    def pulled(pull, n):
        got, cs = [], []
        for k in range(3):
            t = target_ref[3 * n + k]
            c = rank_ref[3 * n + k]
            parts = vec // TAIL
            got.append(jnp.concatenate([pull.near[t, c * parts + i] for i in range(parts)], axis=0))
            cs.append(c_ref[n, k])
        return scale * dot_nt(joined(*got), joined(*cs))

    for n in range(count):
        kh, kl = split2(m[pl.ds(n * size, size), :])
        vh, vl = split2(v_ref[:, n * size : (n + 1) * size])
        u = dot_nn(joined(vh, vh, vl), jnp.concatenate([kh, kl, kh], axis=0))
        u_ref[n] = u
        give(push_w, n, u)
    for o in push_w.order() + [0]:
        push_w.serve(o)
    for n in range(count):
        uh, ul = split2(u_ref[n])
        dh, dl = split2(d_ref[n])
        rest_ref[n] = dot_nn(joined(uh, uh, ul), jnp.concatenate([dh, dl, dh], axis=0))
    for o in push_w.order():
        push_w.advance(o)
    w = push_w.finish().astype(bf16)

    for n in range(count):
        p = dot_nn(w[n * vec : (n + 1) * vec], e_ref[n])
        p_ref[n] = p
        offer(pull_left, n, u_ref[n] - p)
        give(push_p, n, p)
    pull_left.start()
    for o in push_p.order() + [0]:
        push_p.serve(o)
    pull_left.serve(0, -1)
    for s, o in enumerate(push_p.order()):
        push_p.advance(o)
        pull_left.advance(-1, s)
        pull_left.advance(1, s)
    pushed = push_p.finish()
    pull_left.finish()

    for n in range(count):
        sent = pushed[n * vec : (n + 1) * vec]
        q = pulled(pull_left, n) - sent
        t = p_ref[n] + dot_nn(q.astype(bf16), e_ref[n])
        offer(pull_t, n, t)
        rest_ref[n] = rest_ref[n] - sent
    pull_t.start()
    pull_t.serve(0, -1)
    for s in range(layers - 1):
        pull_t.advance(-1, s)
        pull_t.advance(1, s)
    pull_t.finish()

    for n in range(count):
        part = rest_ref[n] - pulled(pull_t, n)
        ph, plow = split2(part)
        kh, kl = split2(m[pl.ds(n * size, size), :])
        result_ref[:, n * size : (n + 1) * size] = dot_nt(
            joined(ph, ph, plow), joined(kh, kl, kh)
        )


def run(geometry, factor, scale, scalars, arrays, row_count, block_size, vec_count):
    total, layers, capacity = geometry
    plane = total // layers
    smem = pl.BlockSpec(memory_space=pltpu.SMEM)
    vmem = pl.BlockSpec(memory_space=pltpu.VMEM)
    dma = pltpu.SemaphoreType.DMA
    pad = -(-row_count // 8) * 8
    block_shape = (row_count, block_size, block_size)
    rows_shape = (row_count, vec_count, block_size)
    scratch = [
        pltpu.VMEM(block_shape, f32),
        pltpu.VMEM(block_shape, bf16),
        pltpu.VMEM(rows_shape, f32),
        pltpu.VMEM(rows_shape, f32),
        pltpu.VMEM(rows_shape, f32),
        pltpu.VMEM((pad * block_size, block_size), f32),
        pltpu.VMEM((PANEL * pad, block_size), f32),
        pltpu.VMEM((PANEL * pad, block_size), f32),
    ]
    vec_tiles = vec_count // TAIL
    pull_count = push_count = 0

    def tiles(*shape):
        return pltpu.VMEM(shape + (TAIL, block_size), bf16)

    for parts, tail in ((block_size // 2 // TAIL, 1), (vec_tiles, 0), (vec_tiles, 0)):
        own, group = row_count * parts + tail, capacity * parts + tail
        pulls = [tiles(own), tiles(layers, plane, group), tiles(total, group)]
        pulls += [tiles(own)] * (2 * layers - 2)
        pulls += [dma((2, layers - 1))] * 2 + [dma((layers, plane))] * 2
        pull_count = len(pulls)
        scratch += pulls
    for _ in range(2):
        group = capacity * vec_tiles
        pushes = [tiles(row_count * 3 * vec_tiles), tiles(total, group), tiles(layers, plane * group)]
        pushes += [pltpu.VMEM((layers - 1, row_count * vec_count, block_size), bf16)] * 2
        pushes += [dma((layers - 1,))] * 2 + [dma((layers, plane))] * 2
        push_count = len(pushes)
        scratch += pushes
    return pl.pallas_call(
        functools.partial(whole_kernel, geometry, factor, scale, (pull_count, push_count)),
        out_shape=jax.ShapeDtypeStruct((vec_count, row_count * block_size), f32),
        in_specs=[smem] * len(scalars) + [vmem] * len(arrays),
        out_specs=vmem,
        scratch_shapes=scratch,
        compiler_params=pltpu.CompilerParams(collective_id=0, has_side_effects=True),
    )(*scalars, *arrays)


def body(diag_noise, couplings, shifts, near_devices, near_slots, vectors):
    dev_count = lax.axis_size("rows")
    my_index = lax.axis_index("rows")
    row_count, block_size = diag_noise.shape[:2]
    vec_count = vectors.shape[0]
    capacity = 3 * row_count // (dev_count - 1) + 2
    layers = LAYERS
    plane = dev_count // layers
    factor = 0.5 / math.sqrt(block_size)
    scale = 0.4 / math.sqrt(block_size)

    target = ((my_index - 1 - near_devices) % dev_count).reshape(-1)
    device_onehot = (target[:, None] == jnp.arange(dev_count, dtype=jnp.int32)[None, :]).astype(
        jnp.int32
    )
    running = jnp.cumsum(device_onehot, axis=0) - 1
    rank = jnp.sum(running * device_onehot, axis=1)
    position = (target % plane * layers + target // plane) * capacity + rank
    every = jnp.arange(dev_count * capacity, dtype=jnp.int32)[:, None]
    hit = position[None, :] == every
    asked = jnp.sum(jnp.where(hit, near_slots.reshape(1, -1) + 1, 0), axis=1) - 1
    hit = (target * capacity + rank)[None, :] == every
    slot = jnp.sum(jnp.where(hit, jnp.arange(3 * row_count, dtype=jnp.int32)[None, :], 0), axis=1)
    groups = [[i * plane + j for j in range(plane)] for i in range(layers)]
    table = lax.all_to_all(
        asked.reshape(plane, layers * capacity), "rows", 0, 0,
        axis_index_groups=groups, tiled=True,
    ).reshape(-1)
    lanes = table.reshape(plane, layers, capacity).transpose(1, 0, 2)
    lanes = jnp.repeat(lanes.reshape(layers, -1), vec_count, axis=1)
    return run(
        (dev_count, layers, capacity), factor, scale,
        (table, slot, target, rank),
        (lanes, diag_noise, shifts.astype(f32), couplings, vectors),
        row_count, block_size, vec_count,
    )


def solution(mesh):
    return jax.shard_map(
        body,
        mesh=mesh,
        in_specs=(
            P("rows", None, None),
            P("rows", None, None, None),
            P("rows", None),
            P("rows", None),
            P("rows", None),
            P(None, "rows"),
        ),
        out_specs=P(None, "rows"),
        check_vma=False,
    )
```

time: 201 us -> 133 us (0.66)
  blocking collectives: 95 us -> 0 us
  Pallas kernels: 46.6 us -> 115 us
  waiting for transfers between devices: 35.9 us -> 2.67 us
  starting transfers between devices: 11.2 us -> 5.2 us
    all_to_all x3 -> x0, blocking collectives: 95 us -> none  [exchange(): x = lax.all_to_all(x, 'rows', split_axis=0, concat_axis=0, tiled=True)]
    pallas_call x6 -> x1, Pallas kernels: 46.6 us -> 115 us  [run(): pl.pallas_call(functools.partial(whole_kernel, geometry, factor, scale, (...]
    all_to_all x2 -> x1, waiting for transfers between devices: 35.9 us -> 2.67 us  [body(): lax.all_to_all(asked.reshape(plane, layers * capacity), 'rows', 0, 0, axi...]
    all_to_all x2 -> x1, starting transfers between devices: 11.2 us -> 5.2 us  [body(): lax.all_to_all(asked.reshape(plane, layers * capacity), 'rows', 0, 0, axi...]
  transfers between devices with their start and end apart: 2 -> 1, of which waited for: 1 -> 1; matrix products, arithmetic and copies ran while one was open for 3% -> 1% of each run, Pallas kernels for 5% -> 0%
where the time goes in v3:
time: 133 us; the launch traced here: 132 us
  Pallas kernels  115 us (86%)
  starting transfers between devices  5.2 us (4%)
  local copies, waits for them, and re-layouts  4.88 us (4%)
  other arithmetic  4.42 us (3%)
  waiting for transfers between devices  2.67 us (2%)
    pallas_call x1, Pallas kernels, run(): pl.pallas_call(functools.partial(whole_kernel, geometry, factor, scale, (...  115 us
    all_to_all x1, starting transfers between devices, body(): lax.all_to_all(asked.reshape(plane, layers * capacity), 'rows', 0, 0, axi...  5.2 us
    all_to_all x1, waiting for transfers between devices, body(): lax.all_to_all(asked.reshape(plane, layers * capacity), 'rows', 0, 0, axi...  2.67 us
  transfers between devices with their start and end apart: 1, of which 1 were waited for; matrix products, arithmetic and copies ran while one was open for 1% of the time, Pallas kernels for 0%

profile of v3, /device:TPU:0, one launch (start us, length us, event | category | flops | bytes accessed | tf_op | source)
XLA Modules:
  0.0 132.5 jit_solution(1674883134025905846)
XLA Ops:
  0.0 0.7 broadcast_add_fusion
  0.7 0.1 copy.21
  0.8 0.1 add.71
  0.9 0.7 add_select_fusion
  1.6 0.1 copy.20
  1.7 0.1 reshape.103.target_ref
  1.8 0.0 copy-start
  1.8 0.1 fusion
  1.8 0.1 reduce_window_sum.11
  1.9 0.2 select_reduce_fusion.2.rank_ref
  2.1 0.0 copy-start.1
  2.1 0.1 select_reduce_fusion.1
  2.2 0.7 sub.31
  2.9 5.2 %all-to-all-start = ((s32[8,1,12]{2,1,0:T(1,128)}), s32[8,1,12]{2,1,0:T(1,128)S(1)}, u32[]{:S(2)}, u32[]{:S(2)}) async-start(s32[8,1,12]{2,1,0:T(1,128)} %bitcast), calls=%async_computation | async-start | bytes 8192 | tf_op jit(solution)/shard_map/all_to_all | solution.py:523
  8.1 0.7 select_reduce_fusion.slot_ref
  8.8 1.3 convert_element_type.7.shift_ref
  10.0 2.7 %all-to-all-done = s32[8,1,12]{2,1,0:T(1,128)S(1)} async-done(((s32[8,1,12]{2,1,0:T(1,128)}), s32[8,1,12]{2,1,0:T(1,128)S(1)}, u32[]{:S(2)}, u32[]{:S(2)}) %all-to-all-start) | async-done | bytes 416 | tf_op jit(solution)/shard_map/all_to_all | solution.py:523
  12.7 0.5 broadcast.117
  13.2 0.7 reduce.3
  13.9 0.6 reshape.104.table_ref
  14.5 0.1 copy.23
  14.6 0.1 copy.24
  14.7 0.1 reshape.105
  14.8 0.1 broadcast_in_dim.29
  14.9 0.7 reshape.106.lanes_ref
  15.6 0.0 copy-done
  15.6 0.0 copy-done.1
  15.6 115.3 %shard_map.64 = f32[32,1792]{1,0:T(8,128)} custom-call(s32[96]{0:T(128)} %reshape.104.table_ref, s32[96]{0:T(128)} %select_reduce_fusion.slot_ref, s32[42]{0:T(128)} %copy-done, s32[42]{0:T(128)} %copy-done.1, s32[4,768]{1,0:T(4,128)} %reshape.106.lanes_ref, bf16[14,128,128]{2,1,0:T(8,128)(2,1)} %noise_ref.1, f32[14,128]{1,0:T(8,128)} %convert_element_type.7.shift_ref, ...), custom_call_target="tpu_custom_call" | custom-call | tf_op jit(solution)/shard_map/pallas_call | solution.py:489
  130.9 1.6 %copy.26 = f32[32,1792]{1,0:T(8,128)} copy(f32[32,1792]{1,0:T(8,128)} %shard_map.64) | data formatting | bytes 458752
  (3 shorter events, 0.0 us)
Async XLA Ops:
  1.8 13.8 %copy-start = (s32[42]{0:T(128)}, s32[42]{0:T(128)S(1)}, u32[]{:S(2)}) copy-start(s32[42]{0:T(128)S(1)} %reshape.103.target_ref) | copy-start | bytes 508
  2.1 13.5 %copy-start.1 = (s32[42]{0:T(128)}, s32[42]{0:T(128)S(1)}, u32[]{:S(2)}) copy-start(s32[42]{0:T(128)S(1)} %select_reduce_fusion.2.rank_ref) | copy-start | bytes 508
  2.9 9.8 %all-to-all-start = ((s32[8,1,12]{2,1,0:T(1,128)}), s32[8,1,12]{2,1,0:T(1,128)S(1)}, u32[]{:S(2)}, u32[]{:S(2)}) async-start(s32[8,1,12]{2,1,0:T(1,128)} %bitcast), calls=%async_computation | async-start | bytes 8192 | tf_op jit(solution)/shard_map/all_to_all | solution.py:523

commit v4 on v3

--- a/solution.py
+++ b/solution.py
@@ -38,7 +38,7 @@
     return lax.dot_general(a, b, (((1,), (1,)), ((), ())), preferred_element_type=f32)
 
 
-def eliminate(m, pscr, qscr, count, pad, size):
+def eliminate(m, pscr, qscr, count, pad, size, hook=None):
     panel = PANEL
     lane = lax.broadcasted_iota(jnp.int32, (pad, size), 1)
     for block in reversed(range(size // panel)):
@@ -61,8 +61,9 @@
                     tile[i, c] = tile[i, c] - tile[i, k] * ratio
             pivot_row = jnp.where(here, 1.0, rows[k])
             scaled = pivot_row * inv
+            step = jnp.where(here, 1.0 + inv, scaled)
             for i in range(k):
-                rows[i] = jnp.where(here, 0.0, rows[i]) - tile[i, k] * scaled
+                rows[i] = rows[i] - tile[i, k] * step
             if block:
                 pscr[pl.ds(k * pad, pad), :] = jnp.where(
                     (lane >= base) & (lane < col), 0.0, pivot_row
@@ -82,6 +83,8 @@
                 update = tdot(left, right)[:base]
                 spot = pl.ds(n * size, base)
                 m[spot, :] = jnp.where(inside, 0.0, m[spot, :]) - update
+        if hook and block * 2 == size // panel:
+            hook()
 
 
 def inside(x, layers):
@@ -156,7 +159,7 @@
             tile = jnp.zeros((TAIL, 128), f32)
             every = source[self.last].astype(f32)
         for c in range(self.capacity):
-            index = jnp.maximum(self.table[(k.qs[e] * k.layers + layer) * self.capacity + c], 0)
+            index = jnp.maximum(self.table[k.qs[e], 0, layer * self.capacity + c], 0)
             for i in range(self.tiles):
                 put(c * self.tiles + i, source[index * self.tiles + i])
             if self.tail:
@@ -193,6 +196,11 @@
             self.serve(d, s)
 
     def finish(self):
+        for layer in range(self.links.layers):
+            for e in range(1, self.links.plane):
+                self.spread(layer, e).wait_recv()
+
+    def drain(self):
         z, layers = self.links.z, self.links.layers
         for d in (-1, 1):
             for s in range(layers - 1):
@@ -201,7 +209,6 @@
                     self.hop(d, s).wait_send()
         for layer in range(layers):
             for e in range(1, self.links.plane):
-                self.spread(layer, e).wait_recv()
                 self.spread(layer, e).wait_send()
 
 
@@ -255,7 +262,7 @@
         arrived = self.arrive[k.zs[o]]
         arrived = arrived.reshape(-1, arrived.shape[-1])
         vec = self.tiles * arrived.shape[0] // (k.plane * self.group)
-        lanes = self.lanes[pl.ds(k.zs[o], 1), :]
+        lanes = self.lanes[k.zs[o]][:1]
         shape = (vec, arrived.shape[0])
         row = lax.broadcasted_iota(jnp.int32, shape, 0)
         col = lax.broadcasted_iota(jnp.int32, shape, 1)
@@ -272,17 +279,52 @@
         for o in self.order():
             self.hop(o).wait_recv()
             total = total + self.zin[o - 1].astype(f32)
+        return total
+
+    def drain(self):
         for o in range(self.links.layers):
             if o:
                 self.hop(o).wait_send()
             for e in range(1, self.links.plane):
                 self.spread(o, e).wait_send()
-        return total
+
+
+def index_kernel(
+    total, layers, capacity, near_ref, target_ref, rank_ref, slot_ref, asked_ref, seen_ref
+):
+    plane = total // layers
+    me = lax.axis_index("rows")
+    width = 3
+    count = near_ref.shape[0] // width
+
+    def clear(i, carry):
+        seen_ref[i] = 0
+        for c in range(capacity):
+            slot_ref[i * capacity + c] = 0
+            asked_ref[i * capacity + c] = -1
+        return carry
+
+    def place(n, carry):
+        for k in range(width):
+            r = n * width + k
+            wanted = near_ref[r]
+            t = me - 1 - wanted // count
+            t = jnp.where(t < 0, t + total, t)
+            c = seen_ref[t]
+            seen_ref[t] = c + 1
+            target_ref[r] = t
+            rank_ref[r] = c
+            slot_ref[t * capacity + c] = r
+            asked_ref[(lax.rem(t, plane) * layers + t // plane) * capacity + c] = lax.rem(wanted, count)
+        return carry
+
+    lax.fori_loop(0, total, clear, 0)
+    lax.fori_loop(0, count, place, 0)
 
 
 def whole_kernel(
     geometry, factor, scale, counts,
-    table_ref, slot_ref, target_ref, rank_ref, lanes_ref, noise_ref, shift_ref, c_ref, v_ref,
+    target_ref, rank_ref, slot_ref, asked_ref, noise_ref, shift_ref, c_ref, v_ref,
     result_ref, *scratch,
 ):
     total, layers, capacity = geometry
@@ -294,11 +336,18 @@
     d_ref, e_ref, u_ref, p_ref, rest_ref, m, pscr, qscr = take(8)
     pad = m.shape[0] // size
     links = Links(total, layers)
-    pull_e = Pull(links, table_ref, capacity, count, 1, take(counts[0]))
-    pull_left = Pull(links, table_ref, capacity, count, 0, take(counts[0]))
-    pull_t = Pull(links, table_ref, capacity, count, 0, take(counts[0]))
-    push_w = Push(links, slot_ref, lanes_ref, capacity, count, take(counts[1]))
-    push_p = Push(links, slot_ref, lanes_ref, capacity, count, take(counts[1]))
+    lanes_ref, ask_out, ask_in, table_ref, ask_send, ask_recv, table_sem = take(7)
+    shares = vec // TAIL
+    split = range(shares)
+
+    def pulls(tails):
+        return [Pull(links, table_ref, capacity, count, tail, take(counts[0])) for tail in tails]
+
+    def pushes():
+        return [Push(links, slot_ref, lanes_ref, capacity, count, take(counts[1])) for _ in split]
+
+    pull_e, pull_left, pull_t = pulls((0, 1)), pulls((0,) * shares), pulls((0,) * shares)
+    push_w, push_p = pushes(), pushes()
 
     barrier = pltpu.get_barrier_semaphore()
     for device in links.partners():
@@ -307,20 +356,47 @@
     row_full = lax.broadcasted_iota(jnp.int32, (size, size), 0)
     col_full = lax.broadcasted_iota(jnp.int32, (size, size), 1)
     on_diag = row_full == col_full
+    shifts = shift_ref[...].astype(f32)
     for n in range(count):
         noise = noise_ref[n].astype(f32)
         d = (noise + noise.T) * (0.5 * factor)
-        d = d + jnp.where(on_diag, shift_ref[pl.ds(n, 1), :], 0.0)
+        d = d + jnp.where(on_diag, shifts[n : n + 1], 0.0)
         d_ref[n] = d
         m[pl.ds(n * size, size), :] = d
         if n < pad - count:
             m[pl.ds((count + n) * size, size), :] = d
-    eliminate(m, pscr, qscr, count, pad, size)
+
+    plane = links.plane
+    asks = layers * capacity
+    ask_lane = lax.broadcasted_iota(jnp.int32, ask_out.shape[1:], 1)
+
+    def ask(e):
+        return links.remote(
+            ask_out.at[links.qs[e]], ask_in.at[links.q], ask_send.at[e], ask_recv.at[e],
+            links.z * plane + links.qs[e],
+        )
+
+    def exchange_asks():
+        for other in range(plane):
+            line = jnp.zeros(ask_out.shape[1:], jnp.int32)
+            for i in range(asks):
+                line = jnp.where(ask_lane == i, asked_ref[other * asks + i], line)
+            ask_out[other] = line
+        pl.semaphore_wait(barrier, len(links.partners()))
+        ask_in[links.q] = ask_out[links.q]
+        for e in range(1, plane):
+            ask(e).start()
+
+    eliminate(m, pscr, qscr, count, pad, size, exchange_asks)
+    for e in range(1, plane):
+        ask(e).wait()
+    table_copy = pltpu.make_async_copy(ask_in, table_ref, table_sem)
+    table_copy.start()
     row = lax.broadcasted_iota(jnp.int32, (half, half), 0)
     col = lax.broadcasted_iota(jnp.int32, (half, half), 1)
     tail_row = lax.broadcasted_iota(jnp.int32, (TAIL, size), 0)
     tile = jnp.zeros((TAIL, size), f32)
-    parts = half // TAIL
+    parts = half // TAIL // 2
     for n in range(count):
         h, low = split2(m[pl.ds(n * size, size), :])
         e = tdot(jnp.concatenate([h, h, low], axis=0), jnp.concatenate([h, low, h], axis=0))
@@ -328,18 +404,33 @@
         left = jnp.where(row >= col, e[:half, :half], e[half:, half:])
         packed = joined(left, e[:half, half:]).astype(bf16)
         for i in range(parts):
-            pull_e.own[n * parts + i] = packed[i * TAIL : (i + 1) * TAIL]
+            for j in range(2):
+                first = (j * parts + i) * TAIL
+                pull_e[j].own[n * parts + i] = packed[first : first + TAIL]
         diag = jnp.sum(jnp.where(on_diag, e, 0.0), axis=0, keepdims=True)
         tile = jnp.where(tail_row == n, diag, tile)
-    pull_e.own[count * parts] = tile.astype(bf16)
-
-    pl.semaphore_wait(barrier, len(links.partners()))
-    pull_e.start()
-    pull_e.serve(0, -1)
+    pull_e[1].own[count * parts] = tile.astype(bf16)
+
+    for pull in pull_e:
+        pull.start()
+    table_copy.wait()
+    for pull in pull_e:
+        pull.serve(0, -1)
+    width = size // TAIL
+    lane = lax.broadcasted_iota(jnp.int32, (8, size), 1) // TAIL
+    for layer in range(layers):
+        for i in range(plane * capacity // width):
+            line = jnp.zeros((8, size), jnp.int32)
+            for j in range(width):
+                other, c = divmod(i * width + j, capacity)
+                line = jnp.where(lane == j, table_ref[other, 0, layer * capacity + c], line)
+            lanes_ref[layer, :, i * size : (i + 1) * size] = line
     for s in range(layers - 1):
-        pull_e.advance(-1, s)
-        pull_e.advance(1, s)
-    pull_e.finish()
+        for pull in pull_e:
+            pull.advance(-1, s)
+            pull.advance(1, s)
+    for pull in pull_e:
+        pull.finish()
 
     def schur(n, carry):
         fs, cs = [], []
@@ -347,9 +438,9 @@
             t = target_ref[3 * n + k]
             c = rank_ref[3 * n + k]
             packed = jnp.concatenate(
-                [pull_e.near[t, c * parts + i] for i in range(parts)], axis=0
+                [pull.near[t, c * parts + i] for pull in pull_e for i in range(parts)], axis=0
             ).astype(f32)
-            tile = pull_e.near[t, capacity * parts].astype(f32)
+            tile = pull_e[1].near[t, capacity * parts].astype(f32)
             diag = jnp.sum(jnp.where(tail_row == c, tile, 0.0), axis=0, keepdims=True)
             flipped = packed.T
             part = packed[:, :half]
@@ -376,22 +467,12 @@
         low = (x * scale).astype(bf16)
         for k in range(3):
             value = dot_nn(low, c_ref[n, k]).astype(bf16)
-            for i in range(vec // TAIL):
-                push.given[(3 * n + k) * (vec // TAIL) + i] = value[i * TAIL : (i + 1) * TAIL]
-
-    def offer(pull, n, x):
-        for i in range(vec // TAIL):
-            pull.own[n * (vec // TAIL) + i] = x[i * TAIL : (i + 1) * TAIL].astype(bf16)
+            for i, part in enumerate(push):
+                part.given[3 * n + k] = value[i * TAIL : (i + 1) * TAIL]
 
     def pulled(pull, n):
-        got, cs = [], []
-        for k in range(3):
-            t = target_ref[3 * n + k]
-            c = rank_ref[3 * n + k]
-            parts = vec // TAIL
-            got.append(jnp.concatenate([pull.near[t, c * parts + i] for i in range(parts)], axis=0))
-            cs.append(c_ref[n, k])
-        return scale * dot_nt(joined(*got), joined(*cs))
+        got = [pull.near[target_ref[3 * n + k], rank_ref[3 * n + k]] for k in range(3)]
+        return scale * dot_nt(joined(*got), joined(*[c_ref[n, k] for k in range(3)]))
 
     for n in range(count):
         kh, kl = split2(m[pl.ds(n * size, size), :])
@@ -399,52 +480,60 @@
         u = dot_nn(joined(vh, vh, vl), jnp.concatenate([kh, kl, kh], axis=0))
         u_ref[n] = u
         give(push_w, n, u)
-    for o in push_w.order() + [0]:
-        push_w.serve(o)
+    for push in push_w:
+        for o in push.order() + [0]:
+            push.serve(o)
     for n in range(count):
         uh, ul = split2(u_ref[n])
         dh, dl = split2(d_ref[n])
         rest_ref[n] = dot_nn(joined(uh, uh, ul), jnp.concatenate([dh, dl, dh], axis=0))
-    for o in push_w.order():
-        push_w.advance(o)
-    w = push_w.finish().astype(bf16)
-
-    for n in range(count):
-        p = dot_nn(w[n * vec : (n + 1) * vec], e_ref[n])
-        p_ref[n] = p
-        offer(pull_left, n, u_ref[n] - p)
-        give(push_p, n, p)
-    pull_left.start()
-    for o in push_p.order() + [0]:
-        push_p.serve(o)
-    pull_left.serve(0, -1)
-    for s, o in enumerate(push_p.order()):
-        push_p.advance(o)
-        pull_left.advance(-1, s)
-        pull_left.advance(1, s)
-    pushed = push_p.finish()
-    pull_left.finish()
-
-    for n in range(count):
-        sent = pushed[n * vec : (n + 1) * vec]
-        q = pulled(pull_left, n) - sent
-        t = p_ref[n] + dot_nn(q.astype(bf16), e_ref[n])
-        offer(pull_t, n, t)
-        rest_ref[n] = rest_ref[n] - sent
-    pull_t.start()
-    pull_t.serve(0, -1)
-    for s in range(layers - 1):
-        pull_t.advance(-1, s)
-        pull_t.advance(1, s)
-    pull_t.finish()
-
-    for n in range(count):
-        part = rest_ref[n] - pulled(pull_t, n)
-        ph, plow = split2(part)
-        kh, kl = split2(m[pl.ds(n * size, size), :])
-        result_ref[:, n * size : (n + 1) * size] = dot_nt(
-            joined(ph, ph, plow), joined(kh, kl, kh)
-        )
+    for push in push_w:
+        for o in push.order():
+            push.advance(o)
+
+    span = [slice(i * TAIL, (i + 1) * TAIL) for i in split]
+    for i in split:
+        w = push_w[i].finish().astype(bf16)
+        for n in range(count):
+            p = dot_nn(w[n * TAIL : (n + 1) * TAIL], e_ref[n])
+            p_ref[n, span[i], :] = p
+            pull_left[i].own[n] = (u_ref[n, span[i], :] - p).astype(bf16)
+            give(push_p[i : i + 1], n, p)
+        pull_left[i].start()
+        for o in push_p[i].order() + [0]:
+            push_p[i].serve(o)
+        pull_left[i].serve(0, -1)
+    for i in split:
+        for s, o in enumerate(push_p[i].order()):
+            push_p[i].advance(o)
+            pull_left[i].advance(-1, s)
+            pull_left[i].advance(1, s)
+    for i in split:
+        pushed = push_p[i].finish()
+        pull_left[i].finish()
+        for n in range(count):
+            sent = pushed[n * TAIL : (n + 1) * TAIL]
+            q = pulled(pull_left[i], n) - sent
+            t = p_ref[n, span[i], :] + dot_nn(q.astype(bf16), e_ref[n])
+            pull_t[i].own[n] = t.astype(bf16)
+            rest_ref[n, span[i], :] = rest_ref[n, span[i], :] - sent
+        pull_t[i].start()
+        pull_t[i].serve(0, -1)
+    for i in split:
+        for s in range(layers - 1):
+            pull_t[i].advance(-1, s)
+            pull_t[i].advance(1, s)
+    for i in split:
+        pull_t[i].finish()
+        for n in range(count):
+            part = rest_ref[n, span[i], :] - pulled(pull_t[i], n)
+            ph, plow = split2(part)
+            kh, kl = split2(m[pl.ds(n * size, size), :])
+            result_ref[span[i], n * size : (n + 1) * size] = dot_nt(
+                joined(ph, ph, plow), joined(kh, kl, kh)
+            )
+    for moved in pull_e + push_w + push_p + pull_left + pull_t:
+        moved.drain()
 
 
 def run(geometry, factor, scale, scalars, arrays, row_count, block_size, vec_count):
@@ -466,23 +555,32 @@
         pltpu.VMEM((PANEL * pad, block_size), f32),
         pltpu.VMEM((PANEL * pad, block_size), f32),
     ]
-    vec_tiles = vec_count // TAIL
+    scratch += [
+        pltpu.VMEM((layers, 8, plane * capacity * TAIL), jnp.int32),
+        pltpu.VMEM((plane, 8, block_size), jnp.int32),
+        pltpu.VMEM((plane, 8, block_size), jnp.int32),
+        pltpu.SMEM((plane, 8, block_size), jnp.int32),
+        dma((plane,)),
+        dma((plane,)),
+        dma,
+    ]
+    shares = vec_count // TAIL
     pull_count = push_count = 0
 
     def tiles(*shape):
         return pltpu.VMEM(shape + (TAIL, block_size), bf16)
 
-    for parts, tail in ((block_size // 2 // TAIL, 1), (vec_tiles, 0), (vec_tiles, 0)):
+    quarter = block_size // 4 // TAIL
+    for parts, tail in ((quarter, 0), (quarter, 1)) + ((1, 0),) * (2 * shares):
         own, group = row_count * parts + tail, capacity * parts + tail
         pulls = [tiles(own), tiles(layers, plane, group), tiles(total, group)]
         pulls += [tiles(own)] * (2 * layers - 2)
         pulls += [dma((2, layers - 1))] * 2 + [dma((layers, plane))] * 2
         pull_count = len(pulls)
         scratch += pulls
-    for _ in range(2):
-        group = capacity * vec_tiles
-        pushes = [tiles(row_count * 3 * vec_tiles), tiles(total, group), tiles(layers, plane * group)]
-        pushes += [pltpu.VMEM((layers - 1, row_count * vec_count, block_size), bf16)] * 2
+    for _ in range(2 * shares):
+        pushes = [tiles(row_count * 3), tiles(total, capacity), tiles(layers, plane * capacity)]
+        pushes += [pltpu.VMEM((layers - 1, row_count * TAIL, block_size), bf16)] * 2
         pushes += [dma((layers - 1,))] * 2 + [dma((layers, plane))] * 2
         push_count = len(pushes)
         scratch += pushes
@@ -498,38 +596,27 @@
 
 def body(diag_noise, couplings, shifts, near_devices, near_slots, vectors):
     dev_count = lax.axis_size("rows")
-    my_index = lax.axis_index("rows")
     row_count, block_size = diag_noise.shape[:2]
     vec_count = vectors.shape[0]
     capacity = 3 * row_count // (dev_count - 1) + 2
     layers = LAYERS
-    plane = dev_count // layers
     factor = 0.5 / math.sqrt(block_size)
     scale = 0.4 / math.sqrt(block_size)
 
-    target = ((my_index - 1 - near_devices) % dev_count).reshape(-1)
-    device_onehot = (target[:, None] == jnp.arange(dev_count, dtype=jnp.int32)[None, :]).astype(
-        jnp.int32
-    )
-    running = jnp.cumsum(device_onehot, axis=0) - 1
-    rank = jnp.sum(running * device_onehot, axis=1)
-    position = (target % plane * layers + target // plane) * capacity + rank
-    every = jnp.arange(dev_count * capacity, dtype=jnp.int32)[:, None]
-    hit = position[None, :] == every
-    asked = jnp.sum(jnp.where(hit, near_slots.reshape(1, -1) + 1, 0), axis=1) - 1
-    hit = (target * capacity + rank)[None, :] == every
-    slot = jnp.sum(jnp.where(hit, jnp.arange(3 * row_count, dtype=jnp.int32)[None, :], 0), axis=1)
-    groups = [[i * plane + j for j in range(plane)] for i in range(layers)]
-    table = lax.all_to_all(
-        asked.reshape(plane, layers * capacity), "rows", 0, 0,
-        axis_index_groups=groups, tiled=True,
-    ).reshape(-1)
-    lanes = table.reshape(plane, layers, capacity).transpose(1, 0, 2)
-    lanes = jnp.repeat(lanes.reshape(layers, -1), vec_count, axis=1)
+    smem = pl.BlockSpec(memory_space=pltpu.SMEM)
+    requests = 3 * row_count
+    lengths = (requests, requests, dev_count * capacity, dev_count * capacity)
+    tables = pl.pallas_call(
+        functools.partial(index_kernel, dev_count, layers, capacity),
+        out_shape=[jax.ShapeDtypeStruct((length,), jnp.int32) for length in lengths],
+        in_specs=[smem],
+        out_specs=[smem] * 4,
+        scratch_shapes=[pltpu.SMEM((dev_count,), jnp.int32)],
+    )((near_devices * row_count + near_slots).reshape(-1))
     return run(
         (dev_count, layers, capacity), factor, scale,
-        (table, slot, target, rank),
-        (lanes, diag_noise, shifts.astype(f32), couplings, vectors),
+        tables,
+        (diag_noise, shifts, couplings, vectors),
         row_count, block_size, vec_count,
     )
 

time: 133 us -> 116 us (0.87)
  starting transfers between devices: 5.2 us -> 0 us
  other arithmetic: 4.42 us -> 0.7 us
  waiting for transfers between devices: 2.67 us -> 0 us
  local copies, waits for them, and re-layouts: 4.88 us -> 2.34 us
  Pallas kernels: 115 us -> 113 us
    all_to_all x1 -> x0, starting transfers between devices: 5.2 us -> none  [body(): lax.all_to_all(asked.reshape(plane, layers * capacity), 'rows', 0, 0, axi...]
    pallas_call x1, Pallas kernels: 115 us -> 111 us  [run(): pl.pallas_call(functools.partial(whole_kernel, geometry, factor, scale, (...]
    all_to_all x1 -> x0, waiting for transfers between devices: 2.67 us -> none  [body(): lax.all_to_all(asked.reshape(plane, layers * capacity), 'rows', 0, 0, axi...]
    pallas_call x0 -> x1, Pallas kernels: none -> 2.25 us  [body(): pl.pallas_call(functools.partial(index_kernel, dev_count, layers, capacit...]
    convert_element_type x2 -> x0, other arithmetic: 1.36 us -> none  [the longest x1 1.28 us: body(): shifts.astype(f32)]
  transfers between devices with their start and end apart: 1 -> 0, of which waited for: 1 -> 0; matrix products, arithmetic and copies ran while one was open for 1% -> 0% of each run, Pallas kernels for 0% -> 0%
where the time goes in v4:
time: 116 us
  Pallas kernels  113 us (97%)
  local copies, waits for them, and re-layouts  2.34 us (2%)
    pallas_call x1, Pallas kernels, run(): pl.pallas_call(functools.partial(whole_kernel, geometry, factor, scale, (...  111 us

profile of v4, /device:TPU:0, one launch (start us, length us, event | category | flops | bytes accessed | tf_op | source)
XLA Modules:
  0.0 115.9 jit_solution(11245649124989569546)
XLA Ops:
  0.0 0.7 multiply_add_fusion
  0.7 0.1 copy.8
  0.8 0.6 reshape.3.near_ref
  1.4 2.3 %shard_map.64 = (s32[42]{0:T(128)}, s32[42]{0:T(128)}, s32[96]{0:T(128)}, s32[96]{0:T(128)}) custom-call(s32[42]{0:T(128)} %reshape.3.near_ref), custom_call_target="tpu_custom_call" | custom-call | tf_op jit(solution)/shard_map/pallas_call | solution.py:609
  3.7 110.6 %shard_map.65 = f32[32,1792]{1,0:T(8,128)} custom-call(s32[42]{0:T(128)} %get-tuple-element.9.target_ref, s32[42]{0:T(128)} %get-tuple-element.10.rank_ref, s32[96]{0:T(128)} %get-tuple-element.11.slot_ref, s32[96]{0:T(128)} %get-tuple-element.12.asked_ref, bf16[14,128,128]{2,1,0:T(8,128)(2,1)} %noise_ref.1, bf16[14,128]{1,0:T(8,128)(2,1)} %shift_ref.1, ...), custom_call_target="tpu_custom_call" | custom-call | tf_op jit(solution)/shard_map/pallas_call | solution.py:587
  114.3 1.6 %copy.10 = f32[32,1792]{1,0:T(8,128)} copy(f32[32,1792]{1,0:T(8,128)} %shard_map.65) | data formatting | bytes 458752

commit v5 on v4

--- a/solution.py
+++ b/solution.py
@@ -13,6 +13,7 @@
 LAYERS = 4
 TAIL = 16
 UNROLL = 7
+STRIDE = 16
 MESH = pl.DeviceIdType.MESH
 bf16, f32 = jnp.bfloat16, jnp.float32
 
@@ -80,7 +81,7 @@
                 qh, qlow = split2(qscr[pl.ds(n, panel, stride=pad), :])
                 right = jnp.concatenate([ph, plow, ph], axis=0)
                 left = jnp.concatenate([qh, qh, qlow], axis=0)
-                update = tdot(left, right)[:base]
+                update = tdot(left[:, :base], right)
                 spot = pl.ds(n * size, base)
                 m[spot, :] = jnp.where(inside, 0.0, m[spot, :]) - update
         if hook and block * 2 == size // panel:
@@ -159,7 +160,7 @@
             tile = jnp.zeros((TAIL, 128), f32)
             every = source[self.last].astype(f32)
         for c in range(self.capacity):
-            index = jnp.maximum(self.table[k.qs[e], 0, layer * self.capacity + c], 0)
+            index = jnp.maximum(self.table.asked(k.qs[e], layer, c), 0)
             for i in range(self.tiles):
                 put(c * self.tiles + i, source[index * self.tiles + i])
             if self.tail:
@@ -213,10 +214,8 @@
 
 
 class Push:
-    def __init__(self, links, slot_ref, lanes_ref, capacity, count, refs):
-        self.links, self.slot, self.lanes, self.capacity, self.count = (
-            links, slot_ref, lanes_ref, capacity, count,
-        )
+    def __init__(self, links, tables, pick_ref, capacity, refs):
+        self.links, self.slot, self.pick, self.capacity = links, tables.slot, pick_ref, capacity
         self.given, self.out, self.arrive, self.zout, self.zin, *sems = refs
         self.z_send, self.z_recv, self.p_send, self.p_recv = sems
         self.group = self.out.shape[1]
@@ -245,7 +244,7 @@
         for e in reversed(range(k.plane)):
             device = k.zs[o] * k.plane + k.qs[e]
             for c in range(self.capacity):
-                index = jnp.maximum(self.slot[device * self.capacity + c], 0)
+                index = self.slot(device * self.capacity + c)
                 for i in range(self.tiles):
                     value = self.given[index * self.tiles + i]
                     if e:
@@ -261,14 +260,7 @@
             self.spread(o, e).wait_recv()
         arrived = self.arrive[k.zs[o]]
         arrived = arrived.reshape(-1, arrived.shape[-1])
-        vec = self.tiles * arrived.shape[0] // (k.plane * self.group)
-        lanes = self.lanes[k.zs[o]][:1]
-        shape = (vec, arrived.shape[0])
-        row = lax.broadcasted_iota(jnp.int32, shape, 0)
-        col = lax.broadcasted_iota(jnp.int32, shape, 1)
-        same = row == lax.rem(col, vec)
-        pick = [jnp.where(same & (lanes == i), 1.0, 0.0).astype(bf16) for i in range(self.count)]
-        return dot_nn(jnp.concatenate(pick, axis=0), arrived)
+        return dot_nn(self.pick[k.zs[o]], arrived)
 
     def advance(self, o):
         self.zout[o - 1] = self.gathered(o).astype(bf16)
@@ -289,42 +281,75 @@
                 self.spread(o, e).wait_send()
 
 
-def index_kernel(
-    total, layers, capacity, near_ref, target_ref, rank_ref, slot_ref, asked_ref, seen_ref
-):
+def spread_requests(ref, buffer):
+    rows, count = ref.shape
+    buffer[...] = jnp.zeros_like(buffer)
+    buffer[0:rows, 0:count] = ref[...] + 1
+    size = buffer.shape[1]
+    total = jnp.zeros((size, size), jnp.int32)
+    for k in range(rows):
+        line = jnp.broadcast_to(buffer[k : k + 1, :], (size, size))
+        total = total + (pltpu.roll(line, k * STRIDE, axis=1) if k else line)
+    return total
+
+
+def index_tables(total, layers, capacity, device_ref, slot_ref, buffer, meta_ref):
     plane = total // layers
-    me = lax.axis_index("rows")
-    width = 3
-    count = near_ref.shape[0] // width
-
-    def clear(i, carry):
-        seen_ref[i] = 0
-        for c in range(capacity):
-            slot_ref[i * capacity + c] = 0
-            asked_ref[i * capacity + c] = -1
-        return carry
-
-    def place(n, carry):
-        for k in range(width):
-            r = n * width + k
-            wanted = near_ref[r]
-            t = me - 1 - wanted // count
-            t = jnp.where(t < 0, t + total, t)
-            c = seen_ref[t]
-            seen_ref[t] = c + 1
-            target_ref[r] = t
-            rank_ref[r] = c
-            slot_ref[t * capacity + c] = r
-            asked_ref[(lax.rem(t, plane) * layers + t // plane) * capacity + c] = lax.rem(wanted, count)
-        return carry
-
-    lax.fori_loop(0, total, clear, 0)
-    lax.fori_loop(0, count, place, 0)
+    size = meta_ref.shape[1]
+    lane = lax.broadcasted_iota(jnp.int32, (size, size), 1)
+    row = lax.broadcasted_iota(jnp.int32, (size, size), 0)
+    devices = spread_requests(device_ref, buffer)
+    wanted = jnp.minimum(spread_requests(slot_ref, buffer), slot_ref.shape[1]).T
+    target = lax.axis_index("rows") - devices
+    target = jnp.where(target < 0, target + total, target)
+    target = jnp.where(devices > 0, target, -1)
+    other = target.T
+    before = jnp.where((target == other) & (row < lane), 1, 0)
+    rank = jnp.minimum(jnp.sum(before, axis=0, keepdims=True), capacity - 1)
+    rank = jnp.broadcast_to(rank, (size, size))
+    lines = [jnp.maximum(target[:1], 0), rank[:1]]
+    rank = rank.T
+    shift = plane.bit_length() - 1
+    ask = ((other & (plane - 1)) * layers + (other >> shift)) * capacity + rank
+    ask = jnp.where(other < 0, -1, ask)
+    spot = jnp.where(other < 0, -1, other * capacity + rank)
+    groups = -(-total * capacity // size)
+    for g in range(groups):
+        here = jnp.where(spot == lane + g * size, row, 0)
+        lines.append(jnp.max(here, axis=0, keepdims=True))
+    for g in range(groups):
+        here = jnp.where(ask == lane + g * size, wanted, 0)
+        lines.append(jnp.max(here, axis=0, keepdims=True) - 1)
+    line_row = lax.broadcasted_iota(jnp.int32, meta_ref.shape, 0)
+    tile = jnp.zeros(meta_ref.shape, jnp.int32)
+    for i, line in enumerate(lines):
+        tile = jnp.where(line_row == i, line, tile)
+    meta_ref[...] = tile
+
+
+class Tables:
+    def __init__(self, links, table_ref, capacity):
+        self.links, self.ref, self.capacity = links, table_ref, capacity
+        self.size = table_ref.shape[2]
+        self.groups = -(-links.layers * links.plane * capacity // self.size)
+
+    def target(self, n, k):
+        return self.ref[self.links.q, 0, k * STRIDE + n]
+
+    def rank(self, n, k):
+        return self.ref[self.links.q, 1, k * STRIDE + n]
+
+    def slot(self, i):
+        return self.ref[self.links.q, 2 + i // self.size, lax.rem(i, self.size)]
+
+    def asked(self, other, layer, c):
+        i = (self.links.q * self.links.layers + layer) * self.capacity + c
+        return self.ref[other, 2 + self.groups + i // self.size, lax.rem(i, self.size)]
 
 
 def whole_kernel(
     geometry, factor, scale, counts,
-    target_ref, rank_ref, slot_ref, asked_ref, noise_ref, shift_ref, c_ref, v_ref,
+    noise_ref, shift_ref, c_source, v_ref, device_ref, slot_ref,
     result_ref, *scratch,
 ):
     total, layers, capacity = geometry
@@ -336,15 +361,19 @@
     d_ref, e_ref, u_ref, p_ref, rest_ref, m, pscr, qscr = take(8)
     pad = m.shape[0] // size
     links = Links(total, layers)
-    lanes_ref, ask_out, ask_in, table_ref, ask_send, ask_recv, table_sem = take(7)
+    pick_ref, buffer, meta_ref, ask_in, table_ref, c_ref = take(6)
+    ask_send, ask_recv, table_sem, c_sem = take(4)
+    c_copy = pltpu.make_async_copy(c_source, c_ref, c_sem)
+    c_copy.start()
+    tables = Tables(links, table_ref, capacity)
     shares = vec // TAIL
     split = range(shares)
 
     def pulls(tails):
-        return [Pull(links, table_ref, capacity, count, tail, take(counts[0])) for tail in tails]
+        return [Pull(links, tables, capacity, count, tail, take(counts[0])) for tail in tails]
 
     def pushes():
-        return [Push(links, slot_ref, lanes_ref, capacity, count, take(counts[1])) for _ in split]
+        return [Push(links, tables, pick_ref, capacity, take(counts[1])) for _ in split]
 
     pull_e, pull_left, pull_t = pulls((0, 1)), pulls((0,) * shares), pulls((0,) * shares)
     push_w, push_p = pushes(), pushes()
@@ -367,23 +396,17 @@
             m[pl.ds((count + n) * size, size), :] = d
 
     plane = links.plane
-    asks = layers * capacity
-    ask_lane = lax.broadcasted_iota(jnp.int32, ask_out.shape[1:], 1)
+    index_tables(total, layers, capacity, device_ref, slot_ref, buffer, meta_ref)
 
     def ask(e):
         return links.remote(
-            ask_out.at[links.qs[e]], ask_in.at[links.q], ask_send.at[e], ask_recv.at[e],
+            meta_ref, ask_in.at[links.q], ask_send.at[e], ask_recv.at[e],
             links.z * plane + links.qs[e],
         )
 
     def exchange_asks():
-        for other in range(plane):
-            line = jnp.zeros(ask_out.shape[1:], jnp.int32)
-            for i in range(asks):
-                line = jnp.where(ask_lane == i, asked_ref[other * asks + i], line)
-            ask_out[other] = line
         pl.semaphore_wait(barrier, len(links.partners()))
-        ask_in[links.q] = ask_out[links.q]
+        ask_in[links.q] = meta_ref[...]
         for e in range(1, plane):
             ask(e).start()
 
@@ -417,14 +440,18 @@
     for pull in pull_e:
         pull.serve(0, -1)
     width = size // TAIL
-    lane = lax.broadcasted_iota(jnp.int32, (8, size), 1) // TAIL
+    lane = lax.broadcasted_iota(jnp.int32, (TAIL, size), 1)
+    same = lax.broadcasted_iota(jnp.int32, (TAIL, size), 0) == lax.rem(lane, TAIL)
+    lane = lane // TAIL
     for layer in range(layers):
         for i in range(plane * capacity // width):
-            line = jnp.zeros((8, size), jnp.int32)
+            line = jnp.zeros((TAIL, size), jnp.int32)
             for j in range(width):
                 other, c = divmod(i * width + j, capacity)
-                line = jnp.where(lane == j, table_ref[other, 0, layer * capacity + c], line)
-            lanes_ref[layer, :, i * size : (i + 1) * size] = line
+                line = jnp.where(lane == j, tables.asked(other, layer, c), line)
+            for n in range(count):
+                chosen = jnp.where(same & (line == n), 1.0, 0.0).astype(bf16)
+                pick_ref[layer, n * TAIL : (n + 1) * TAIL, i * size : (i + 1) * size] = chosen
     for s in range(layers - 1):
         for pull in pull_e:
             pull.advance(-1, s)
@@ -432,11 +459,13 @@
     for pull in pull_e:
         pull.finish()
 
+    c_copy.wait()
+
     def schur(n, carry):
         fs, cs = [], []
         for k in range(3):
-            t = target_ref[3 * n + k]
-            c = rank_ref[3 * n + k]
+            t = tables.target(n, k)
+            c = tables.rank(n, k)
             packed = jnp.concatenate(
                 [pull.near[t, c * parts + i] for pull in pull_e for i in range(parts)], axis=0
             ).astype(f32)
@@ -468,10 +497,10 @@
         for k in range(3):
             value = dot_nn(low, c_ref[n, k]).astype(bf16)
             for i, part in enumerate(push):
-                part.given[3 * n + k] = value[i * TAIL : (i + 1) * TAIL]
+                part.given[k * STRIDE + n] = value[i * TAIL : (i + 1) * TAIL]
 
     def pulled(pull, n):
-        got = [pull.near[target_ref[3 * n + k], rank_ref[3 * n + k]] for k in range(3)]
+        got = [pull.near[tables.target(n, k), tables.rank(n, k)] for k in range(3)]
         return scale * dot_nt(joined(*got), joined(*[c_ref[n, k] for k in range(3)]))
 
     for n in range(count):
@@ -536,11 +565,11 @@
         moved.drain()
 
 
-def run(geometry, factor, scale, scalars, arrays, row_count, block_size, vec_count):
+def run(geometry, factor, scale, arrays, row_count, block_size, vec_count):
     total, layers, capacity = geometry
     plane = total // layers
-    smem = pl.BlockSpec(memory_space=pltpu.SMEM)
     vmem = pl.BlockSpec(memory_space=pltpu.VMEM)
+    apart = pl.BlockSpec(memory_space=pl.ANY)
     dma = pltpu.SemaphoreType.DMA
     pad = -(-row_count // 8) * 8
     block_shape = (row_count, block_size, block_size)
@@ -556,12 +585,15 @@
         pltpu.VMEM((PANEL * pad, block_size), f32),
     ]
     scratch += [
-        pltpu.VMEM((layers, 8, plane * capacity * TAIL), jnp.int32),
-        pltpu.VMEM((plane, 8, block_size), jnp.int32),
+        pltpu.VMEM((layers, row_count * TAIL, plane * capacity * TAIL), bf16),
+        pltpu.VMEM((8, block_size), jnp.int32),
+        pltpu.VMEM((8, block_size), jnp.int32),
         pltpu.VMEM((plane, 8, block_size), jnp.int32),
         pltpu.SMEM((plane, 8, block_size), jnp.int32),
+        pltpu.VMEM((row_count, 3, block_size, block_size), bf16),
         dma((plane,)),
         dma((plane,)),
+        dma,
         dma,
     ]
     shares = vec_count // TAIL
@@ -579,7 +611,7 @@
         pull_count = len(pulls)
         scratch += pulls
     for _ in range(2 * shares):
-        pushes = [tiles(row_count * 3), tiles(total, capacity), tiles(layers, plane * capacity)]
+        pushes = [tiles(3 * STRIDE), tiles(total, capacity), tiles(layers, plane * capacity)]
         pushes += [pltpu.VMEM((layers - 1, row_count * TAIL, block_size), bf16)] * 2
         pushes += [dma((layers - 1,))] * 2 + [dma((layers, plane))] * 2
         push_count = len(pushes)
@@ -587,11 +619,11 @@
     return pl.pallas_call(
         functools.partial(whole_kernel, geometry, factor, scale, (pull_count, push_count)),
         out_shape=jax.ShapeDtypeStruct((vec_count, row_count * block_size), f32),
-        in_specs=[smem] * len(scalars) + [vmem] * len(arrays),
+        in_specs=[vmem, vmem, apart, vmem, vmem, vmem],
         out_specs=vmem,
         scratch_shapes=scratch,
         compiler_params=pltpu.CompilerParams(collective_id=0, has_side_effects=True),
-    )(*scalars, *arrays)
+    )(*arrays)
 
 
 def body(diag_noise, couplings, shifts, near_devices, near_slots, vectors):
@@ -603,20 +635,9 @@
     factor = 0.5 / math.sqrt(block_size)
     scale = 0.4 / math.sqrt(block_size)
 
-    smem = pl.BlockSpec(memory_space=pltpu.SMEM)
-    requests = 3 * row_count
-    lengths = (requests, requests, dev_count * capacity, dev_count * capacity)
-    tables = pl.pallas_call(
-        functools.partial(index_kernel, dev_count, layers, capacity),
-        out_shape=[jax.ShapeDtypeStruct((length,), jnp.int32) for length in lengths],
-        in_specs=[smem],
-        out_specs=[smem] * 4,
-        scratch_shapes=[pltpu.SMEM((dev_count,), jnp.int32)],
-    )((near_devices * row_count + near_slots).reshape(-1))
     return run(
         (dev_count, layers, capacity), factor, scale,
-        tables,
-        (diag_noise, shifts, couplings, vectors),
+        (diag_noise, shifts, couplings, vectors, near_devices.T, near_slots.T),
         row_count, block_size, vec_count,
     )
 

time: 116 us -> 111 us (0.957)
  Pallas kernels: 113 us -> 110 us
    pallas_call x1 -> x0, Pallas kernels: 2.25 us -> none  [body(): pl.pallas_call(functools.partial(index_kernel, dev_count, layers, capacit...]
where the time goes in v5:
time: 111 us
  Pallas kernels  110 us (99%)
  local copies, waits for them, and re-layouts  1.64 us (1%)
    pallas_call x1, Pallas kernels, run(): pl.pallas_call(functools.partial(whole_kernel, geometry, factor, scale, (...  110 us

profile of v5, /device:TPU:0, one launch (start us, length us, event | category | flops | bytes accessed | tf_op | source)
XLA Modules:
  0.0 111.4 jit_solution(3840098741988561261)
XLA Ops:
  0.0 109.8 %shard_map.64 = f32[32,1792]{1,0:T(8,128)} custom-call(bf16[14,128,128]{2,1,0:T(8,128)(2,1)} %noise_ref.1, bf16[14,128]{1,0:T(8,128)(2,1)} %shift_ref.1, bf16[14,3,128,128]{3,2,1,0:T(8,128)(2,1)} %c_source.1, f32[32,1792]{1,0:T(8,128)} %v_ref.1, s32[3,14]{1,0:T(4,128)} %bitcast.2, s32[3,14]{1,0:T(4,128)} %bitcast.3), custom_call_target="tpu_custom_call" | custom-call | tf_op jit(solution)/shard_map/pallas_call | solution.py:619
  109.8 1.6 %copy.8 = f32[32,1792]{1,0:T(8,128)} copy(f32[32,1792]{1,0:T(8,128)} %shard_map.64) | data formatting | bytes 458752
